TPU v7x, 512 devices: a whole 4x4x16 slice. The times are simulated.
512 devices in a mesh: seq: 64 (over z, y), tp: 8 (over x, core).
Axes of the slice: x: 4, y: 4, z: 16, core: 2. Of those that a mesh axis runs over, the one named last changes fastest.
Arguments:
- residual: bfloat16 [8192, 8192], P('seq', 'tp'), may hold values from -6 to 6
- steer_table: bfloat16 [7, 8192], P(None, 'tp'), may hold values from -6 to 6
- steer_index: int32 [4], replicated, may hold values from 0 to 6
- steer_num: int32 [4], replicated, may hold values from -8 to 8
- lengths: int32 [4], replicated, may hold values from 1 to 4096, 8192 in all
- queries: bfloat16 [8192, 64, 128], P('seq', 'tp'), may hold values from -128 to 128
- keys: bfloat16 [8192, 8, 128], P('seq', 'tp'), may hold values from -6 to 6
- values: bfloat16 [8192, 8, 128], P('seq', 'tp'), may hold values from -6 to 6
- inner_x: bfloat16 [8192, 16384], P('seq', 'tp'), may hold values from -6 to 6
- dt_raw: bfloat16 [8192, 16384], P('seq', 'tp'), may hold values from -4 to 4
- dt_bias: float32 [16384], P('tp'), may hold values from -7 to -2.5
- a_log: float32 [16, 16384], P(None, 'tp'), may hold values from -2.3 to 2.77
- skip_gain: float32 [16384], P('tp'), may hold values from 0.5 to 1.5
- bc_weight: bfloat16 [32, 16384], P(None, 'tp'), may hold values from -0.046875 to 0.046875
Outputs:
- steered: bfloat16 [8192, 8192], P('seq', 'tp')
- context: bfloat16 [8192, 64, 128], P('seq', 'tp')
- mixed: bfloat16 [8192, 16384], P('seq', 'tp')
Inputs may be any that keep to these rules, and one draw needn't show every extreme that they name: `lengths`: the 4 requests lie end to end in token order and the longest has exactly 8192 // 2 tokens. `steer_num`: a request's steering multiplier is its numerator over 4.
All inputs are finite; a program needn't handle non-finite values.
Results may differ from a plain program's by a relative error of at most 0.0039.
Values may be sent and summed in bfloat16 or wider, within the bound.
A program may use at most 128 MiB of HBM per device.

v0:
```python
import jax
import jax.numpy as jnp
from jax import lax
from jax.sharding import PartitionSpec as P

NEG_FILL = -1e30
KEY_BLOCK = 512


def prefix(part, axis, combine, identity):
    place = lax.axis_index(axis)
    gathered = jax.tree.map(lambda a: lax.all_gather(a, axis), part)
    state = jax.tree.map(lambda a, e: jnp.zeros_like(a) + jnp.asarray(e, a.dtype), part, identity)

    def one(lap, state):
        return combine(
            state, jax.tree.map(lambda a: lax.dynamic_index_in_dim(a, lap, 0, False), gathered)
        )

    return lax.fori_loop(0, place, one, state)


def request_bounds(lengths, positions):
    seg_ends = jnp.cumsum(lengths)
    seg_starts = seg_ends - lengths
    member = (positions[:, None] >= seg_starts[None, :]) & (positions[:, None] < seg_ends[None, :])
    member_int = member.astype(jnp.int32)
    req_start = jnp.sum(member_int * seg_starts[None, :], axis=1)
    return (member_int, req_start)


def chain_combine(earlier, later):
    return (earlier[0] * later[0], later[0] * earlier[1] + later[1])


def shards(
    residual,
    steer_table,
    steer_index,
    steer_num,
    lengths,
    queries,
    keys,
    values,
    inner_x,
    dt_raw,
    dt_bias,
    a_log,
    skip_gain,
    bc_weight,
):
    tok_rows = residual.shape[0]
    positions = lax.axis_index("seq") * tok_rows + jnp.arange(tok_rows, dtype=jnp.int32)
    member_int, req_start = request_bounds(lengths, positions)
    vector_pick = (
        steer_index[:, None] == jnp.arange(steer_table.shape[0], dtype=jnp.int32)[None, :]
    ).astype(jnp.float32)
    vector_pick = vector_pick * (steer_num.astype(jnp.float32) * 0.25)[:, None]
    token_pick = jnp.dot(
        member_int.astype(jnp.float32), vector_pick, precision=lax.Precision.HIGHEST
    )
    steer_add = jnp.dot(
        token_pick, steer_table.astype(jnp.float32), precision=lax.Precision.HIGHEST
    )
    steered = (residual.astype(jnp.float32) + steer_add).astype(jnp.bfloat16)
    local_heads = queries.shape[1]
    local_kv = keys.shape[1]
    head_dim = queries.shape[2]
    head_group = local_heads // local_kv
    score_scale = 1.0 / head_dim**0.5
    grouped_q = queries.reshape(tok_rows, local_kv, head_group, head_dim)

    def update(carried, key_part, value_part, key_start):
        run_max, run_total, run_acc = carried
        count = key_part.shape[0]
        scores = (
            jnp.einsum("tkgd,skd->tkgs", grouped_q, key_part, preferred_element_type=jnp.float32)
            * score_scale
        )
        key_pos = key_start + jnp.arange(count, dtype=jnp.int32)
        allowed = (key_pos[None, :] <= positions[:, None]) & (
            key_pos[None, :] >= req_start[:, None]
        )
        allowed = allowed[:, None, None, :]
        masked = jnp.where(allowed, scores, NEG_FILL)
        new_max = jnp.maximum(run_max, jnp.max(masked, axis=-1))
        expo = jnp.where(allowed, jnp.exp(masked - new_max[..., None]), 0.0)
        rescale = jnp.exp(run_max - new_max)
        weights = expo.astype(jnp.bfloat16)
        run_total = run_total * rescale + jnp.sum(expo, axis=-1)
        products = jnp.einsum(
            "tkgs,skd->tkgd", weights, value_part, preferred_element_type=jnp.float32
        )
        run_acc = run_acc * rescale[..., None] + products
        return (new_max, run_total, run_acc)

    start_state = (
        jnp.full((tok_rows, local_kv, head_group), NEG_FILL, jnp.float32),
        jnp.zeros((tok_rows, local_kv, head_group), jnp.float32),
        jnp.zeros((tok_rows, local_kv, head_group, head_dim), jnp.float32),
    )
    key_piece = lax.all_gather(keys, "seq", axis=0, tiled=True)
    value_piece = lax.all_gather(values, "seq", axis=0, tiled=True)
    count = key_piece.shape[0]
    blocks = count // KEY_BLOCK
    key_blocks = key_piece.reshape(blocks, KEY_BLOCK, local_kv, head_dim)
    value_blocks = value_piece.reshape(blocks, KEY_BLOCK, local_kv, head_dim)

    def block_step(inner_state, item):
        block_index, key_part, value_part = item
        return (update(inner_state, key_part, value_part, block_index * KEY_BLOCK), None)

    final_state, _ = lax.scan(
        block_step, start_state, (jnp.arange(blocks, dtype=jnp.int32), key_blocks, value_blocks)
    )
    final_max, final_total, final_acc = final_state
    context = (
        (final_acc / final_total[..., None])
        .astype(jnp.bfloat16)
        .reshape(tok_rows, local_heads, head_dim)
    )
    partial_bc = jnp.einsum("tc,jc->tj", inner_x, bc_weight, preferred_element_type=jnp.float32)
    summed_bc = lax.psum(partial_bc, "tp")
    state_size = a_log.shape[0]
    b_rows = summed_bc[:, :state_size]
    c_rows = summed_bc[:, state_size:]
    keep_rows = jnp.where(positions == req_start, 0.0, 1.0).astype(jnp.float32)
    rates = jnp.exp(a_log)
    step_sizes = jax.nn.softplus(dt_raw.astype(jnp.float32) + dt_bias[None, :])
    x_float = inner_x.astype(jnp.float32)

    def local_step(carried, item):
        decay_total, state_now = carried
        step_row, x_row, b_row, keep_row = item
        factor = jnp.exp(-step_row[None, :] * rates) * keep_row
        state_now = factor * state_now + (step_row * x_row)[None, :] * b_row[:, None]
        return ((decay_total * factor, state_now), None)

    ones_state = jnp.ones(rates.shape, jnp.float32)
    zero_state = jnp.zeros(rates.shape, jnp.float32)
    (decay_total, end_state), _ = lax.scan(
        local_step, (ones_state, zero_state), (step_sizes, x_float, b_rows, keep_rows), unroll=8
    )
    incoming = prefix((decay_total, end_state), "seq", chain_combine, (ones_state, zero_state))[1]

    def output_step(state_now, item):
        step_row, x_row, b_row, c_row, keep_row = item
        factor = jnp.exp(-step_row[None, :] * rates) * keep_row
        state_now = factor * state_now + (step_row * x_row)[None, :] * b_row[:, None]
        out_row = jnp.sum(c_row[:, None] * state_now, axis=0) + skip_gain * x_row
        return (state_now, out_row.astype(jnp.bfloat16))

    _, mixed = lax.scan(
        output_step, incoming, (step_sizes, x_float, b_rows, c_rows, keep_rows), unroll=8
    )
    return (steered, context, mixed)


def solution(mesh):
    return jax.shard_map(
        shards,
        mesh=mesh,
        in_specs=(
            P("seq", "tp"),
            P(None, "tp"),
            P(),
            P(),
            P(),
            P("seq", "tp", None),
            P("seq", "tp", None),
            P("seq", "tp", None),
            P("seq", "tp"),
            P("seq", "tp"),
            P("tp"),
            P(None, "tp"),
            P("tp"),
            P(None, "tp"),
        ),
        out_specs=(P("seq", "tp"), P("seq", "tp", None), P("seq", "tp")),
        check_vma=False,
    )
```

profile of v0, /device:TPU:504, one launch (start us, length us, event | category | flops | bytes accessed | tf_op | source)
XLA Modules:
  0.0 902.7 jit_solution(4664678258861879669)
XLA Ops:
  13.0 25.6 %psum.7 = f32[128,32]{0,1:T(8,128)S(1)} all-reduce(f32[128,32]{0,1:T(8,128)S(1)} %fusion.102), channel_id=1, replica_groups=mesh['seq'=64,'tp'=8] {'tp'}, use_global_device_ids=true, to_apply=%region_6.7 | all-reduce | flops 4096 | bytes 32768 | tf_op jit(solution)/shard_map/psum | solution.py:123
  39.4 180.9 %while.55 = (s32[]{:T(128)}, f32[16,2048]{1,0:T(8,128)S(1)}, f32[16,2048]{1,0:T(8,128)S(1)}, f32[16,8,2048]{2,1,0:T(8,128)S(1)}, f32[16,2048]{1,0:T(8,128)S(1)},...) while((s32[]{:T(128)}, f32[16,2048]{1,0:T(8,128)S(1)}, ...), condition=%wide.region_8.9_spmd.clone, body=%wide.region_7.8_spmd.clone.sunk | while | flops 2195466 | bytes 1248228 | solution.py:141
  40.3 5.3 fusion.130
  45.6 5.2 fusion.129
  51.6 5.3 fusion.130
  56.9 5.2 fusion.129
  62.9 5.3 fusion.130
  68.2 5.2 fusion.129
  74.2 5.3 fusion.130
  85.5 5.3 fusion.130
  90.8 5.2 fusion.129
  96.8 5.3 fusion.130
  102.1 5.2 fusion.129
  108.2 5.3 fusion.130
  113.4 5.2 fusion.129
  119.5 5.3 fusion.130
  130.8 5.3 fusion.130
  142.1 5.3 fusion.130
  153.4 5.3 fusion.130
  164.7 5.3 fusion.130
  176.0 5.3 fusion.130
  181.3 5.2 fusion.129
  187.3 5.3 fusion.130
  192.6 5.2 fusion.129
  198.6 5.3 fusion.130
  209.9 5.3 fusion.130
  226.1 61.9 %all-gather.9.cloned.1.call-done = bf16[8192,1,128]{2,0,1:T(8,128)(2,1)} async-done(((bf16[128,1,128]{2,0,1:T(8,128)(2,1)}), bf16[8192,1,128]{2,0,1:T(8,128)(2,1)}) %all-gather.9.cloned.1.call-update) | async-done | bytes 2097168 | tf_op jit(solution)/shard_map/all_gather | solution.py:103
  288.1 78.5 %while.54 = (s32[]{:T(128)}, f32[128,1,8]{0,2,1:T(8,128)S(1)}, f32[128,1,8]{0,2,1:T(8,128)S(1)}, f32[128,1,8,128]{0,3,2,1:T(8,128)S(1)}, s32[16]{0:T(128)S(1)}, ...) while((s32[]{:T(128)}, f32[128,1,8]{0,2,1:T(8,128)S(1)}, ...), condition=%wide.region_5.6_spmd.clone, body=%wide.region_2.5_spmd.clone.sunk | while | flops 275847808 | bytes 8198825 | solution.py:113
  367.8 74.9 %all-gather.11.cloned.1.call-done = f32[1024,2048]{1,0:T(8,128)} async-done(((f32[16,2048]{1,0:T(8,128)}), f32[1024,2048]{1,0:T(8,128)}) %all-gather.11.cloned.1.call-update) | async-done | bytes 8388624 | tf_op jit(solution)/shard_map/all_gather | solution.py:12
  442.7 153.9 %all-gather.13.cloned.1.call-done = f32[1024,2048]{1,0:T(8,128)} async-done(((f32[16,2048]{1,0:T(8,128)}), f32[1024,2048]{1,0:T(8,128)}) %all-gather.13.cloned.1.call-update) | async-done | bytes 8388624 | tf_op jit(solution)/shard_map/all_gather | solution.py:12
  596.6 67.0 %while.52 = (s32[]{:T(128)}, f32[16,2048]{1,0:T(8,128)S(1)}, s32[]{:T(128)}, f32[64,16,2048]{2,1,0:T(8,128)}, f32[64,16,2048]{2,1,0:T(8,128)}, /*index=5*/s32[]{:T(128)}, s32[]{:T(128)}, s32[]{:T(128)}) while((s32[]{:T(128)}, f32[16,2048]{1,0:T(8,128)S(1)}, s32[]{:T(128)}, f32[64,16,2048]{2,1,0:T(8,128)}, f32[64,16,2048]{2,1,0:T(8,128)}, ...), condition=%wide.region_10.11_spmd, body=%wide.region_9.10_spmd.sunk | while | flops 65541 | bytes 524411 | solution.py:20
  663.6 232.7 %while.53 = (s32[]{:T(128)}, f32[16,2048]{1,0:T(8,128)S(1)}, bf16[16,8,2048]{2,1,0:T(8,128)(2,1)}, f32[16,8,2048]{2,1,0:T(8,128)}, f32[16,2048]{1,0:T(8,128)S(1)...) while((s32[]{:T(128)}, f32[16,2048]{1,0:T(8,128)S(1)}, ...), condition=%wide.region_20.21_spmd, body=%wide.region_11.20_spmd.sunk | while | flops 2883593 | bytes 1915265 | solution.py:153
  (565 shorter events, 434.1 us)
Async XLA Ops:
  7.2 4.5 copy-start
  7.2 31.6 %copy-start.8 = (f32[16,2048]{1,0:T(8,128)S(1)}, f32[16,2048]{1,0:T(8,128)}, u32[]{:S(2)}) copy-start(f32[16,2048]{1,0:T(8,128)} %param.33) | copy-start | bytes 393220
  7.2 31.6 %copy-start.4 = (bf16[128,2048]{1,0:T(8,128)(2,1)S(1)}, bf16[128,2048]{1,0:T(8,128)(2,1)}, u32[]{:S(2)}) copy-start(bf16[128,2048]{1,0:T(8,128)(2,1)} %param.31) | copy-start | bytes 1572868
  7.2 31.6 %copy-start.10 = (f32[2048]{0:T(1024)S(1)}, f32[2048]{0:T(1024)}, u32[]{:S(2)}) copy-start(f32[2048]{0:T(1024)} %param.32) | copy-start | bytes 24580
  7.2 218.9 %all-gather.7.cloned.1.call-start = ((), (), s32[]{:S(2)}) async-start(), calls=%async_computation | async-start | bytes 2129920 | tf_op jit(solution)/shard_map/all_gather | solution.py:102
  7.9 280.1 %all-gather.9.cloned.1.call-start = ((), (), s32[]{:S(2)}) async-start(), calls=%async_computation.1 | async-start | bytes 2129920 | tf_op jit(solution)/shard_map/all_gather | solution.py:103
  8.7 434.0 %all-gather.11.cloned.1.call-start = ((), (), s32[]{:S(2)}) async-start(), calls=%async_computation.2 | async-start | bytes 8519680 | tf_op jit(solution)/shard_map/all_gather | solution.py:12
  10.3 2.7 copy-start.11
  39.4 183.0 %copy-start.5 = (bf16[128,8,128]{2,1,0:T(8,128)(2,1)S(1)}, bf16[128,8,128]{2,1,0:T(8,128)(2,1)}, u32[]{:S(2)}) copy-start(bf16[128,8,128]{2,1,0:T(8,128)(2,1)} %param.27) | copy-start | bytes 786436
  220.3 0.7 copy-start.9
  220.4 0.7 copy-start.1
  220.4 1.3 copy-start.7
  220.4 67.7 %copy-start.2 = (f32[16,8,2048]{2,1,0:T(8,128)}, f32[16,8,2048]{2,1,0:T(8,128)S(1)}, u32[]{:S(2)}) copy-start(f32[16,8,2048]{2,1,0:T(8,128)S(1)} %get-tuple-element.1075) | copy-start | bytes 3145732
  220.4 67.7 %copy-start.3 = (f32[16,8,2048]{2,1,0:T(8,128)}, f32[16,8,2048]{2,1,0:T(8,128)S(1)}, u32[]{:S(2)}) copy-start(f32[16,8,2048]{2,1,0:T(8,128)S(1)} %get-tuple-element.1076) | copy-start | bytes 3145732
  221.0 375.5 %all-gather.13.cloned.1.call-start = ((), (), s32[]{:S(2)}) async-start(), calls=%async_computation.3 | async-start | bytes 8519680 | tf_op jit(solution)/shard_map/all_gather | solution.py:12
  366.8 296.7 %copy-start.6 = (f32[2048]{0:T(1024)S(1)}, f32[2048]{0:T(1024)}, u32[]{:S(2)}) copy-start(f32[2048]{0:T(1024)} %param.34) | copy-start | bytes 24580
Sparse Core Ops, SparseCore 0:
  11.0 137.2 all-gather.6
  151.2 136.8 all-gather.8
  291.0 151.6 all-gather.10
  445.5 151.0 all-gather.12
where the time goes:
time: 912 us; the launch traced here: 903 us
  other arithmetic  449 us (49%)
  waiting for transfers between devices  293 us (32%)
  local copies, waits for them, and re-layouts  56.6 us (6%)
  matrix products  52.2 us (6%)
  blocking collectives  25.6 us (3%)
  between operations  14.1 us (2%)
  loops' own time  12.7 us (1%)
    all_gather x2, waiting for transfers between devices, prefix(): gathered = jax.tree.map(lambda a: lax.all_gather(a, axis), part)  229 us
    reduce_sum x48, other arithmetic, output_step(): out_row = jnp.sum(c_row[:, None] * state_now, axis=0) + skip_gain * x_row  147 us
    add x16, other arithmetic, local_step(): factor * state_now + (step_row * x_row)[None, :] * b_row[:, None]  84.3 us
    mul x16, other arithmetic, local_step(): return ((decay_total * factor, state_now), None)  82.6 us
    add x63, other arithmetic, chain_combine(): return (earlier[0] * later[0], later[0] * earlier[1] + later[1])  65.4 us
    all_gather x1, waiting for transfers between devices, shards(): value_piece = lax.all_gather(values, 'seq', axis=0, tiled=True)  61.9 us
    mul x16, other arithmetic, output_step(): step_row * x_row  29.2 us
    dot_general x16, matrix products, update(): jnp.einsum('tkgs,skd->tkgd', weights, value_part, preferred_element_type=...  26 us
  transfers between devices with their start and end apart: 4, of which 3 were waited for; matrix products, arithmetic and copies ran while one was open for 29% of the time, Pallas kernels for 0%

commit v1 on v0

v1 whole, which is shorter than its diff:
```python
import functools
import jax
import jax.numpy as jnp
from jax import lax
from jax.experimental import pallas as pl
from jax.experimental.pallas import tpu as pltpu
from jax.sharding import PartitionSpec as P

LOG2E = 1.4426950408889634
NEG_FILL = -1e30
RESET = 1e30
YN = 4
ZN = 16
SEQ = YN * ZN
TPN = 8
WIN = 8
TOK = 128
GROUP = 16
MESH = pl.DeviceIdType.MESH
F32 = jnp.float32
BF16 = jnp.bfloat16


def gather_kernel(kv_ref, x_ref, w_ref, win_ref, bc_ref, parts, own_sem, zs, zr, rs, rr, ls, lr, ks, kr, vs, vr, bs, br):
    seq = lax.axis_index("seq")
    tp = lax.axis_index("tp")
    z = seq // YN
    y = lax.rem(seq, YN)
    left_y = lax.rem(y + YN - 1, YN)
    right_y = lax.rem(y + 1, YN)
    up = lax.rem(z + 1, ZN) * YN + y
    down = lax.rem(z + ZN - 1, ZN) * YN + y
    right = z * YN + right_y
    left = z * YN + left_y
    far_y = lax.rem(y + 2, YN)

    barrier = pltpu.get_barrier_semaphore()
    for peer in (up, down, right, left):
        pl.semaphore_signal(barrier, inc=1, device_id=(peer, tp), device_id_type=MESH)
    for off in range(1, TPN):
        pl.semaphore_signal(barrier, inc=1, device_id=(seq, lax.rem(tp + off, TPN)), device_id_type=MESH)
    pl.semaphore_wait(barrier, 4 + TPN - 1)

    def remote(src, dst, ssem, rsem, peer):
        return pltpu.make_async_remote_copy(
            src_ref=src, dst_ref=dst, send_sem=ssem, recv_sem=rsem, device_id=(peer, tp), device_id_type=MESH
        )

    def block(s):
        return kv_ref if s == 0 else win_ref.at[s, y]

    def z_copy(s):
        return remote(block(s - 1), win_ref.at[s, y], zs.at[s], zr.at[s], up)

    def right_copy(s):
        return remote(block(s), win_ref.at[s, y], rs.at[s], rr.at[s], right)

    def left_copy(s):
        return remote(block(s), win_ref.at[s, y], ls.at[s], lr.at[s], left)

    def k_copy(s):
        return remote(win_ref.at[s, left_y, 0], win_ref.at[s, left_y, 0], ks.at[s], kr.at[s], right)

    def v_copy(s):
        return remote(win_ref.at[s, right_y, 1], win_ref.at[s, right_y, 1], vs.at[s], vr.at[s], left)

    own = pltpu.make_async_copy(kv_ref, win_ref.at[0, y], own_sem)
    z_copy(1).start()
    right_copy(0).start()
    left_copy(0).start()
    own.start()

    parts[tp] = lax.dot_general(w_ref[...], x_ref[...], (((1,), (1,)), ((), ())), preferred_element_type=F32)

    def bc_copy(off):
        return pltpu.make_async_remote_copy(
            src_ref=parts.at[tp], dst_ref=parts.at[tp], send_sem=bs.at[off], recv_sem=br.at[off],
            device_id=(seq, lax.rem(tp + off, TPN)), device_id_type=MESH,
        )

    for off in range(1, TPN):
        bc_copy(off).start()

    for s in range(1, WIN + 1):
        z_copy(s).wait_recv()
        if s < WIN:
            z_copy(s + 1).start()
        right_copy(s).start()
        left_copy(s).start()
        right_copy(s - 1).wait_recv()
        k_copy(s - 1).start()
        left_copy(s - 1).wait_recv()
        v_copy(s - 1).start()
    right_copy(WIN).wait_recv()
    k_copy(WIN).start()
    left_copy(WIN).wait_recv()
    v_copy(WIN).start()
    for off in range(1, TPN):
        bc_copy(off).wait()
    total = parts[0]
    for t in range(1, TPN):
        total = total + parts[t]
    bc_ref[...] = total
    own.wait()
    for s in range(WIN + 1):
        if s > 0:
            z_copy(s).wait_send()
        right_copy(s).wait_send()
        left_copy(s).wait_send()
        k_copy(s).wait()
        v_copy(s).wait()


def gather(kv, x, w):
    vm = pl.BlockSpec(memory_space=pltpu.VMEM)
    dma = pltpu.SemaphoreType.DMA
    n = WIN + 1
    return pl.pallas_call(
        gather_kernel,
        out_shape=(
            jax.ShapeDtypeStruct((n, YN, 2, TOK, 128), BF16),
            jax.ShapeDtypeStruct((32, TOK), F32),
        ),
        in_specs=[vm, vm, vm],
        out_specs=(pl.BlockSpec(memory_space=pl.ANY), vm),
        scratch_shapes=[pltpu.VMEM((TPN, 32, TOK), F32), dma(())] + [dma((n,)) for _ in range(10)] + [dma((TPN,)), dma((TPN,))],
        compiler_params=pltpu.CompilerParams(collective_id=0, has_side_effects=True),
        name="gather_kv_bc",
    )(kv, x, w)


def log1p_exp(v):
    return jnp.maximum(v, 0.0) + jnp.log1p(jnp.exp(-jnp.abs(v)))


def fill_group(g, dt_ref, x_ref, bias, rates_unused, keep_ref, step_s, u_s):
    rows = pl.ds(pl.multiple_of(g * GROUP, GROUP), GROUP)
    raw = dt_ref[rows, :].astype(F32)
    x = x_ref[rows, :].astype(F32)
    step = log1p_exp(raw + bias)
    u_s[...] = (step * x).reshape(GROUP, 16, 128)
    step_s[...] = (step + keep_ref[rows, 0:1]).reshape(GROUP, 16, 128)
    return x


def local_kernel(bc_ref, dt_ref, x_ref, bias_ref, alog_ref, add_ref, tile_ref, rate_s, step_s, u_s, state_s, sum_s):
    rate_s[...] = (jnp.exp(alog_ref[...]) * (-LOG2E)).reshape(16, 16, 128)
    state_s[...] = jnp.zeros_like(state_s)
    sum_s[...] = jnp.zeros_like(sum_s)
    bias = bias_ref[...]

    @pl.loop(0, TOK // GROUP)
    def _(g):
        fill_group(g, dt_ref, x_ref, bias, None, add_ref, step_s, u_s)

        def token(t, carry):
            states, total = carry
            st = step_s[t]
            u = u_s[t]
            p = g * GROUP + t
            new = []
            for n in range(16):
                f = jnp.exp2(st * rate_s[n])
                new.append(f * states[n] + u * bc_ref[n, p])
            return tuple(new), total + st

        states, total = lax.fori_loop(0, GROUP, token, (tuple(state_s[n] for n in range(16)), sum_s[...]))
        for n in range(16):
            state_s[n] = states[n]
        sum_s[...] = total

    total = sum_s[...]
    for n in range(16):
        s = state_s[n]
        for q in range(4):
            tile_ref[n * 4 + q, 0:4, :] = s[4 * q : 4 * q + 4]
            tile_ref[n * 4 + q, 4:8, :] = total[4 * q : 4 * q + 4]


def local_pass(bc, dt, x, bias, a_log, reset_add):
    vm = pl.BlockSpec(memory_space=pltpu.VMEM)
    sm = pl.BlockSpec(memory_space=pltpu.SMEM)
    return pl.pallas_call(
        local_kernel,
        out_shape=jax.ShapeDtypeStruct((SEQ, 8, 128), F32),
        in_specs=[sm, vm, vm, vm, vm, vm],
        out_specs=vm,
        scratch_shapes=[
            pltpu.VMEM((16, 16, 128), F32),
            pltpu.VMEM((GROUP, 16, 128), F32),
            pltpu.VMEM((GROUP, 16, 128), F32),
            pltpu.VMEM((16, 16, 128), F32),
            pltpu.VMEM((16, 128), F32),
        ],
        name="scan_local",
    )(bc, dt, x, bias, a_log, reset_add)


def exchange_kernel(tile_ref, rate_ref, inc_ref, got, back, ret, s1, r1, s2, r2, l1, l2):
    seq = lax.axis_index("seq")
    tp = lax.axis_index("tp")
    barrier = pltpu.get_barrier_semaphore()

    def peer(off):
        return lax.rem(seq + off, SEQ)

    def hello(off, c):
        pl.semaphore_signal(barrier, inc=1, device_id=(peer(off), tp), device_id_type=MESH)
        return c

    lax.fori_loop(1, SEQ, hello, 0)
    pl.semaphore_wait(barrier, SEQ - 1)

    def out_copy(off):
        return pltpu.make_async_remote_copy(
            src_ref=tile_ref.at[peer(off)], dst_ref=got.at[seq], send_sem=s1.at[off], recv_sem=r1.at[off],
            device_id=(peer(off), tp), device_id_type=MESH,
        )

    def back_copy(off):
        return pltpu.make_async_remote_copy(
            src_ref=back.at[peer(off)], dst_ref=ret.at[seq], send_sem=s2.at[off], recv_sem=r2.at[off],
            device_id=(peer(off), tp), device_id_type=MESH,
        )

    def run(fn):
        def body(off, c):
            fn(off)
            return c

        lax.fori_loop(1, SEQ, body, 0)

    mine = pltpu.make_async_copy(tile_ref.at[seq], got.at[seq], l1)
    mine.start()
    run(lambda off: out_copy(off).start())
    mine.wait()
    run(lambda off: out_copy(off).wait_recv())

    rate = rate_ref[...]

    def chunk(i, state):
        back[i] = state
        tile = got[i]
        return jnp.exp2(tile[4:8] * rate) * state + tile[0:4]

    lax.fori_loop(0, SEQ, chunk, jnp.zeros((4, 128), F32), unroll=4)

    mine2 = pltpu.make_async_copy(back.at[seq], ret.at[seq], l2)
    mine2.start()
    run(lambda off: back_copy(off).start())
    mine2.wait()
    run(lambda off: back_copy(off).wait_recv())
    inc_ref[...] = ret[...]
    run(lambda off: out_copy(off).wait_send())
    run(lambda off: back_copy(off).wait_send())


def exchange(tiles, rate):
    vm = pl.BlockSpec(memory_space=pltpu.VMEM)
    dma = pltpu.SemaphoreType.DMA
    return pl.pallas_call(
        exchange_kernel,
        out_shape=jax.ShapeDtypeStruct((SEQ, 4, 128), F32),
        in_specs=[vm, vm],
        out_specs=vm,
        scratch_shapes=[
            pltpu.VMEM((SEQ, 8, 128), F32),
            pltpu.VMEM((SEQ, 4, 128), F32),
            pltpu.VMEM((SEQ, 4, 128), F32),
        ]
        + [dma((SEQ,)) for _ in range(4)]
        + [dma(()), dma(())],
        compiler_params=pltpu.CompilerParams(collective_id=1, has_side_effects=True),
        name="state_exchange",
    )(tiles, rate)


def final_kernel(bc_ref, dt_ref, x_ref, bias_ref, alog_ref, add_ref, skip_ref, inc_ref, out_ref, rate_s, step_s, u_s, state_s, y_s):
    rate_s[...] = (jnp.exp(alog_ref[...]) * (-LOG2E)).reshape(16, 16, 128)
    for n in range(16):
        for q in range(4):
            state_s[n, 4 * q : 4 * q + 4] = inc_ref[n * 4 + q]
    bias = bias_ref[...]
    skip = skip_ref[...]

    @pl.loop(0, TOK // GROUP)
    def _(g):
        x = fill_group(g, dt_ref, x_ref, bias, None, add_ref, step_s, u_s)

        def token(t, states):
            st = step_s[t]
            u = u_s[t]
            p = g * GROUP + t
            new = []
            acc = None
            for n in range(16):
                f = jnp.exp2(st * rate_s[n])
                s = f * states[n] + u * bc_ref[n, p]
                new.append(s)
                term = s * bc_ref[16 + n, p]
                acc = term if acc is None else acc + term
            y_s[t] = acc
            return tuple(new)

        states = lax.fori_loop(0, GROUP, token, tuple(state_s[n] for n in range(16)))
        for n in range(16):
            state_s[n] = states[n]
        rows = pl.ds(pl.multiple_of(g * GROUP, GROUP), GROUP)
        x = x_ref[rows, :].astype(F32)
        out_ref[rows, :] = (y_s[...].reshape(GROUP, 2048) + skip * x).astype(BF16)


def final_pass(bc, dt, x, bias, a_log, reset_add, skip, inc):
    vm = pl.BlockSpec(memory_space=pltpu.VMEM)
    sm = pl.BlockSpec(memory_space=pltpu.SMEM)
    return pl.pallas_call(
        final_kernel,
        out_shape=jax.ShapeDtypeStruct(x.shape, BF16),
        in_specs=[sm] + [vm] * 7,
        out_specs=vm,
        scratch_shapes=[
            pltpu.VMEM((16, 16, 128), F32),
            pltpu.VMEM((GROUP, 16, 128), F32),
            pltpu.VMEM((GROUP, 16, 128), F32),
            pltpu.VMEM((16, 16, 128), F32),
            pltpu.VMEM((GROUP, 16, 128), F32),
        ],
        name="scan_final",
    )(bc, dt, x, bias, a_log, reset_add, skip, inc)


ROWS = 256
PLANE = YN * TOK


def attend_kernel(meta_ref, q_ref, win_ref, res_ref, table_ref, ctx_ref, st_ref):
    z = meta_ref[0]
    base = meta_ref[1]
    first_start = meta_ref[2]
    planes = z - first_start // PLANE + 1
    scale = LOG2E / 128.0**0.5

    @pl.loop(0, 1024 // ROWS)
    def _(rt):
        rows = pl.ds(pl.multiple_of(rt * ROWS, ROWS), ROWS)
        q = q_ref[rows, :]
        pos = base + rt * (ROWS // 8) + lax.broadcasted_iota(jnp.int32, (ROWS, 1), 0) // 8
        start = jnp.zeros((ROWS, 1), jnp.int32)
        for r in range(4):
            start = jnp.where(pos >= meta_ref[4 + r], meta_ref[4 + r], start)

        def step(dz, carry):
            m, l, acc = carry
            k = win_ref[dz, :, 0].reshape(PLANE, 128)
            v = win_ref[dz, :, 1].reshape(PLANE, 128)
            s = lax.dot_general(q, k, (((1,), (1,)), ((), ())), preferred_element_type=F32)
            key_pos = (z - dz) * PLANE + lax.broadcasted_iota(jnp.int32, (1, PLANE), 1)
            ok = (key_pos <= pos) & (key_pos >= start)
            s = jnp.where(ok, s, NEG_FILL)
            m_new = jnp.maximum(m, jnp.max(s, axis=1, keepdims=True))
            e = jnp.exp2((s - m_new) * scale)
            fix = jnp.exp2((m - m_new) * scale)
            l = l * fix + jnp.sum(e, axis=1, keepdims=True)
            acc = acc * fix + jnp.dot(e.astype(BF16), v, preferred_element_type=F32)
            return m_new, l, acc

        init = (
            jnp.full((ROWS, 1), NEG_FILL, F32),
            jnp.zeros((ROWS, 1), F32),
            jnp.zeros((ROWS, 128), F32),
        )
        m, l, acc = lax.fori_loop(0, planes, step, init)
        ctx_ref[rows, :] = (acc / l).astype(BF16)

    tpos = base + lax.broadcasted_iota(jnp.int32, (TOK, 1), 0)
    add = jnp.zeros((TOK, 1024), F32)
    for r in range(4):
        vec = table_ref[pl.ds(meta_ref[8 + r], 1), :] * (meta_ref[12 + r].astype(F32) * 0.25)
        add = jnp.where(tpos >= meta_ref[4 + r], vec, add)
    st_ref[...] = (res_ref[...].astype(F32) + add).astype(BF16)


def attend(meta, q, win, residual, table):
    vm = pl.BlockSpec(memory_space=pltpu.VMEM)
    sm = pl.BlockSpec(memory_space=pltpu.SMEM)
    return pl.pallas_call(
        attend_kernel,
        out_shape=(jax.ShapeDtypeStruct(q.shape, BF16), jax.ShapeDtypeStruct(residual.shape, BF16)),
        in_specs=[sm, vm, vm, vm, vm],
        out_specs=(vm, vm),
        name="attend_steer",
    )(meta, q, win, residual, table)


def shards(residual, steer_table, steer_index, steer_num, lengths, queries, keys, values, inner_x, dt_raw, dt_bias, a_log, skip_gain, bc_weight):
    seq = lax.axis_index("seq")
    base = seq * TOK
    ends = jnp.cumsum(lengths).astype(jnp.int32)
    starts = ends - lengths
    positions = base + jnp.arange(TOK, dtype=jnp.int32)
    is_reset = jnp.any(positions[:, None] == starts[None, :], axis=1)
    reset_add = jnp.where(is_reset, RESET, 0.0).astype(F32)[:, None]
    first_start = jnp.max(jnp.where(starts <= base, starts, 0))
    meta = jnp.concatenate(
        [jnp.stack([seq // YN, base, first_start, 0]).astype(jnp.int32), starts, steer_index, steer_num]
    )
    kv = jnp.stack([keys[:, 0], values[:, 0]])
    win, bc = gather(kv, inner_x, bc_weight)
    bias = dt_bias[None, :]
    tiles = local_pass(bc, dt_raw, inner_x, bias, a_log, reset_add)
    rate = lax.dynamic_slice(a_log, (seq // 4, lax.rem(seq, 4) * 512), (1, 512)).reshape(4, 128)
    inc = exchange(tiles, jnp.exp(rate) * (-LOG2E))
    mixed = final_pass(bc, dt_raw, inner_x, bias, a_log, reset_add, skip_gain[None, :], inc)
    ctx, steered = attend(meta, queries.reshape(1024, 128), win, residual, steer_table.astype(F32))
    return steered, ctx.reshape(queries.shape), mixed


def solution(mesh):
    return jax.shard_map(
        shards,
        mesh=mesh,
        in_specs=(
            P("seq", "tp"),
            P(None, "tp"),
            P(),
            P(),
            P(),
            P("seq", "tp", None),
            P("seq", "tp", None),
            P("seq", "tp", None),
            P("seq", "tp"),
            P("seq", "tp"),
            P("tp"),
            P(None, "tp"),
            P("tp"),
            P(None, "tp"),
        ),
        out_specs=(P("seq", "tp"), P("seq", "tp", None), P("seq", "tp")),
        check_vma=False,
    )
```

time: 912 us -> 136 us (0.15)
  the two profiles are of different devices: /device:TPU:504 before, /device:TPU:8 now
where the time goes in v1:
time: 136 us
  Pallas kernels  126 us (93%)
  other arithmetic  6.34 us (5%)
  local copies, waits for them, and re-layouts  2.64 us (2%)
    pallas_call x1, Pallas kernels, gather(): pl.pallas_call(gather_kernel, out_shape=(jax.ShapeDtypeStruct((n, YN, 2,...  54.2 us
    pallas_call x1, Pallas kernels, exchange(): pl.pallas_call(exchange_kernel, out_shape=jax.ShapeDtypeStruct((SEQ, 4, 1...  48.5 us
    pallas_call x1, Pallas kernels, final_pass(): pl.pallas_call(final_kernel, out_shape=jax.ShapeDtypeStruct(x.shape, BF16...  10.3 us
    pallas_call x1, Pallas kernels, local_pass(): pl.pallas_call(local_kernel, out_shape=jax.ShapeDtypeStruct((SEQ, 8, 128)...  7.96 us
    pallas_call x1, Pallas kernels, attend(): pl.pallas_call(attend_kernel, out_shape=(jax.ShapeDtypeStruct(q.shape, BF...  5.03 us

profile of v1, /device:TPU:8, one launch (start us, length us, event | category | flops | bytes accessed | tf_op | source)
XLA Modules:
  0.0 135.6 jit_solution(15330275291550604842)
XLA Ops:
  0.6 0.8 reduce-window.9
  1.5 1.3 fusion
  2.8 1.9 %concatenate.3.meta_ref = s32[16]{0:T(128)} concatenate(s32[1]{0:T(128)} %bitcast, s32[1]{0:T(128)} %bitcast.1, s32[1]{0:T(128)} %bitcast.4, s32[1]{0:T(128)} %constant.40.clone.1, s32[4]{0:T(128)S(1)} %get-tuple-element.12, s32[4]{0:T(128)} %param.16, s32[4]{0:T(128)} %param.17), dimensions={0} | concatenate | bytes 128 | tf_op jit(solution)/shard_map/concatenate | solution.py:404
  4.7 1.4 %pad_maximum_fusion.kv_ref = bf16[2,128,128]{2,1,0:T(8,128)(2,1)} fusion(bf16[1,128,128]{2,1,0:T(8,128)(2,1)} %bitcast.19, bf16[1,128,128]{2,1,0:T(8,128)(2,1)} %bitcast.20), kind=kLoop, calls=%fused_computation | loop fusion | flops 32768 | bytes 131072 | tf_op jit(solution)/shard_map/stack | solution.py:407
  6.1 54.2 %gather_kv_bc.1 = (bf16[9,4,2,128,128]{4,3,2,1,0:T(8,128)(2,1)}, f32[32,128]{1,0:T(8,128)}) custom-call(bf16[2,128,128]{2,1,0:T(8,128)(2,1)} %pad_maximum_fusion.kv_ref, bf16[128,2048]{1,0:T(8,128)(2,1)} %x_ref.5, bf16[32,2048]{1,0:T(8,128)(2,1)} %w_ref.1), custom_call_target="tpu_custom_call" | custom-call | tf_op jit(solution)/shard_map/gather_kv_bc/pallas_call | solution.py:118
  60.3 1.3 convert_element_type.3.table_ref
  61.6 5.0 %attend_steer.1 = (bf16[1024,128]{1,0:T(8,128)(2,1)}, bf16[128,1024]{1,0:T(8,128)(2,1)}) custom-call(s32[16]{0:T(128)} %concatenate.3.meta_ref, bf16[1024,128]{1,0:T(8,128)(2,1)} %bitcast.16, bf16[9,4,2,128,128]{4,3,2,1,0:T(8,128)(2,1)} %get-tuple-element.7.win_ref, bf16[128,1024]{1,0:T(8,128)(2,1)} %res_ref.1, f32[7,1024]{1,0:T(8,128)} %convert_element_type.3.table_ref), custom_call_target="tpu_custom_call" | custom-call | tf_op jit(solution)/shard_map/attend_steer/pallas_call | solution.py:386
  66.7 0.1 compare_reduce_fusion
  66.8 0.7 copy.20.add_ref
  67.5 8.0 %scan_local.1.tile_ref = f32[64,8,128]{2,1,0:T(8,128)} custom-call(f32[32,128]{1,0:T(8,128)} %get-tuple-element.10.bc_ref, bf16[128,2048]{1,0:T(8,128)(2,1)} %dt_ref.3, bf16[128,2048]{1,0:T(8,128)(2,1)} %x_ref.5, f32[1,2048]{1,0:T(1,128)} %bitcast.17, f32[16,2048]{1,0:T(8,128)} %alog_ref.3, f32[128,1]{1,0:T(8,128)} %copy.20.add_ref), custom_call_target="tpu_custom_call" | custom-call | tf_op jit(solution)/shard_map/scan_local/pallas_call | solution.py:183
  75.5 1.4 %exponential_multiply_fusion = f32[1,512]{1,0:T(1,128)} fusion(f32[16,2048]{1,0:T(8,128)} %alog_ref.3, s32[]{:T(128)S(6)} %select_n.34, s32[]{:T(128)S(6)} %select_n.35), kind=kLoop, calls=%fused_computation.2 | loop fusion | flops 512 | bytes 4104 | tf_op jit(solution)/shard_map/mul | solution.py:412
  76.8 48.5 %state_exchange.1.inc_ref = f32[64,4,128]{2,1,0:T(4,128)} custom-call(f32[64,8,128]{2,1,0:T(8,128)} %scan_local.1.tile_ref, f32[4,128]{1,0:T(4,128)} %bitcast.22), custom_call_target="tpu_custom_call" | custom-call | tf_op jit(solution)/shard_map/state_exchange/pallas_call | solution.py:261
  125.3 10.3 %scan_final.1 = bf16[128,2048]{1,0:T(8,128)(2,1)} custom-call(f32[32,128]{1,0:T(8,128)} %get-tuple-element.10.bc_ref, bf16[128,2048]{1,0:T(8,128)(2,1)} %dt_ref.3, bf16[128,2048]{1,0:T(8,128)(2,1)} %x_ref.5, f32[1,2048]{1,0:T(1,128)} %bitcast.18, f32[16,2048]{1,0:T(8,128)} %alog_ref.3, f32[128,1]{1,0:T(8,128)} %copy.20.add_ref, f32[1,2048]{1,0:T(1,128)} %bitcast.21, ...), custom_call_target="tpu_custom_call" | custom-call | tf_op jit(solution)/shard_map/scan_final/pallas_call | solution.py:316
  (2 shorter events, 0.0 us)

commit v2 on v1

v2 whole, which is shorter than its diff:
```python
import functools
import jax
import jax.numpy as jnp
from jax import lax
from jax.experimental import pallas as pl
from jax.experimental.pallas import tpu as pltpu
from jax.sharding import PartitionSpec as P

LOG2E = 1.4426950408889634
NEG_FILL = -1e30
RESET = 1e30
YN = 4
ZN = 16
SEQ = YN * ZN
TPN = 8
WIN = 8
TOK = 128
GROUP = 16
MESH = pl.DeviceIdType.MESH
F32 = jnp.float32
BF16 = jnp.bfloat16


def starts_of(len_ref):
    s1 = len_ref[0]
    s2 = s1 + len_ref[1]
    s3 = s2 + len_ref[2]
    return (jnp.int32(0), s1, s2, s3)


def log1p_exp(v):
    return jnp.maximum(v, 0.0) + jnp.log1p(jnp.exp(-jnp.abs(v)))


def fill_group(g, base, starts, dt_ref, x_ref, bias, step_s, u_s):
    rows = pl.ds(pl.multiple_of(g * GROUP, GROUP), GROUP)
    raw = dt_ref[rows, :].astype(F32)
    x = x_ref[rows, :].astype(F32)
    step = log1p_exp(raw + bias)
    pos = base + g * GROUP + lax.broadcasted_iota(jnp.int32, (GROUP, 1), 0)
    hit = (pos == starts[0]) | (pos == starts[1]) | (pos == starts[2]) | (pos == starts[3])
    u_s[...] = (step * x).reshape(GROUP, 16, 128)
    step_s[...] = (step + jnp.where(hit, RESET, 0.0)).reshape(GROUP, 16, 128)


def main_kernel(
    len_ref, k_ref, v_ref, x_ref, w_ref, dt_ref, bias_ref, alog_ref,
    win_ref, bc_ref, inc_ref,
    parts, bc_s, rate_s, step_s, u_s, msg, ych, zout, zin, outb, inc_s,
    own_sem, bc_sem, zs, zr, rs, rr, ls, lr, ks, kr, vs, vr, bs, br, ps, pr, qs, qr, fs, fr,
):
    seq = lax.axis_index("seq")
    tp = lax.axis_index("tp")
    z = seq // YN
    y = lax.rem(seq, YN)
    left_y = lax.rem(y + YN - 1, YN)
    right_y = lax.rem(y + 1, YN)

    def zy(dz, dy):
        return lax.rem(z + dz, ZN) * YN + lax.rem(y + dy, YN)

    up = zy(1, 0)
    right = zy(0, 1)
    left = zy(0, YN - 1)

    barrier = pltpu.get_barrier_semaphore()
    for dz in (1, 2, 4, ZN - 1, ZN - 2, ZN - 4):
        pl.semaphore_signal(barrier, inc=1, device_id=(zy(dz, 0), tp), device_id_type=MESH)
    for dy in range(1, YN):
        pl.semaphore_signal(barrier, inc=1, device_id=(zy(0, dy), tp), device_id_type=MESH)
    for off in range(1, TPN):
        pl.semaphore_signal(barrier, inc=1, device_id=(seq, lax.rem(tp + off, TPN)), device_id_type=MESH)
    pl.semaphore_wait(barrier, 6 + YN - 1 + TPN - 1)

    def remote(src, dst, ssem, rsem, peer):
        return pltpu.make_async_remote_copy(
            src_ref=src, dst_ref=dst, send_sem=ssem, recv_sem=rsem, device_id=(peer, tp), device_id_type=MESH
        )

    def block(s, h):
        return (k_ref, v_ref)[h] if s == 0 else win_ref.at[s, y, h]

    def z_copy(s, h):
        return remote(block(s - 1, h), win_ref.at[s, y, h], zs.at[h, s], zr.at[h, s], up)

    def right_copy(s, h):
        return remote(block(s, h), win_ref.at[s, y, h], rs.at[h, s], rr.at[h, s], right)

    def left_copy(s, h):
        return remote(block(s, h), win_ref.at[s, y, h], ls.at[h, s], lr.at[h, s], left)

    def k_copy(s):
        return remote(win_ref.at[s, left_y, 0], win_ref.at[s, left_y, 0], ks.at[s], kr.at[s], right)

    def v_copy(s):
        return remote(win_ref.at[s, right_y, 1], win_ref.at[s, right_y, 1], vs.at[s], vr.at[s], left)

    def spread(s):
        right_copy(s - 1, 0).wait_recv()
        k_copy(s - 1).start()
        left_copy(s - 1, 1).wait_recv()
        v_copy(s - 1).start()

    def kv_step(s):
        for h in (0, 1):
            z_copy(s, h).wait_recv()
            if s < WIN:
                z_copy(s + 1, h).start()
            right_copy(s, h).start()
            left_copy(s, h).start()
        spread(s)

    own = [pltpu.make_async_copy((k_ref, v_ref)[h], win_ref.at[0, y, h], own_sem.at[h]) for h in (0, 1)]
    for h in (0, 1):
        z_copy(1, h).start()
    for h in (0, 1):
        right_copy(0, h).start()
        left_copy(0, h).start()
        own[h].start()

    parts[tp] = lax.dot_general(w_ref[...], x_ref[...], (((1,), (1,)), ((), ())), preferred_element_type=F32)

    def bc_copy(off):
        return pltpu.make_async_remote_copy(
            src_ref=parts.at[tp], dst_ref=parts.at[tp], send_sem=bs.at[off], recv_sem=br.at[off],
            device_id=(seq, lax.rem(tp + off, TPN)), device_id_type=MESH,
        )

    for off in range(1, TPN):
        bc_copy(off).start()

    rate_s[...] = (jnp.exp(alog_ref[...]) * (-LOG2E)).reshape(16, 16, 128)
    msg[...] = jnp.zeros_like(msg)
    bias = bias_ref[...]
    base = seq * TOK
    starts = starts_of(len_ref)
    kv_step(1)
    for off in range(1, TPN):
        bc_copy(off).wait_recv()
    total_bc = parts[0]
    for t in range(1, TPN):
        total_bc = total_bc + parts[t]
    bc_ref[...] = total_bc
    to_smem = pltpu.make_async_copy(bc_ref, bc_s, bc_sem)
    to_smem.start()
    to_smem.wait()

    def scan_groups(lo, hi):
        @pl.loop(lo, hi)
        def _(g):
            fill_group(g, base, starts, dt_ref, x_ref, bias, step_s, u_s)

            def token(t, carry):
                states, total = carry
                st = step_s[t]
                u = u_s[t]
                p = g * GROUP + t
                new = []
                for n in range(16):
                    f = jnp.exp2(st * rate_s[n])
                    new.append(f * states[n] + u * bc_s[n, p])
                return tuple(new), total + st

            init = (tuple(msg[n // 4, n % 4] for n in range(16)), msg[0, 4])
            states, total = lax.fori_loop(0, GROUP, token, init, unroll=2)
            for n in range(16):
                msg[n // 4, n % 4] = states[n]
            msg[0, 4] = total

    scan_groups(0, 3)
    kv_step(2)
    scan_groups(3, 6)
    kv_step(3)
    scan_groups(6, 8)
    total = msg[0, 4]
    for q in range(1, 4):
        msg[q, 4] = total

    def part_copy(d):
        return remote(msg.at[lax.rem(y + d, YN)], ych.at[y], ps.at[d], pr.at[d], zy(0, d))

    for d in (1, 3, 2):
        part_copy(d).start()
    ych[y] = msg[y]
    kv_step(4)
    for d in range(1, YN):
        part_copy(d).wait_recv()
    rate = rate_s[pl.ds(4 * y, 4)]
    acc = ych[0, 0:4]
    dec = ych[0, 4]
    for c in range(1, YN):
        acc = jnp.exp2(rate * ych[c, 4][None]) * acc + ych[c, 0:4]
        dec = dec + ych[c, 4]

    def z_round(j, d):
        return remote(zout.at[j], zin.at[j], qs.at[j], qr.at[j], zy(d, 0))

    for j, d in enumerate((1, 1, 2, 4)):
        zout[j, 0:4] = acc
        zout[j, 4] = dec
        z_round(j, d).start()
        kv_step(5 + j)
        z_round(j, d).wait_recv()
        here = (z >= d).astype(F32)
        got = zin[j, 0:4] * here
        got_dec = zin[j, 4] * here
        if j == 0:
            acc, dec = got, got_dec
        else:
            acc = acc + jnp.exp2(rate * dec[None]) * got
            dec = dec + got_dec

    for c in range(YN):
        outb[c] = acc
        if c < YN - 1:
            acc = jnp.exp2(rate * ych[c, 4][None]) * acc + ych[c, 0:4]

    def back_copy(d):
        return remote(outb.at[lax.rem(y + d, YN)], inc_s.at[y], fs.at[d], fr.at[d], zy(0, d))

    for d in (1, 3, 2):
        back_copy(d).start()
    inc_s[y] = outb[y]
    spread(WIN + 1)
    for d in range(1, YN):
        back_copy(d).wait_recv()
    inc_ref[...] = inc_s[...]

    for h in (0, 1):
        own[h].wait()
    for off in range(1, TPN):
        bc_copy(off).wait_send()
    for d in range(1, YN):
        part_copy(d).wait_send()
        back_copy(d).wait_send()
    for j, d in enumerate((1, 1, 2, 4)):
        z_round(j, d).wait_send()
    for s in range(WIN + 1):
        for h in (0, 1):
            if s > 0:
                z_copy(s, h).wait_send()
            right_copy(s, h).wait_send()
            left_copy(s, h).wait_send()
        right_copy(s, 1).wait_recv()
        left_copy(s, 0).wait_recv()
        k_copy(s).wait()
        v_copy(s).wait()


def main_pass(lengths, k, v, x, w, dt, bias, a_log):
    vm = pl.BlockSpec(memory_space=pltpu.VMEM)
    sm = pl.BlockSpec(memory_space=pltpu.SMEM)
    dma = pltpu.SemaphoreType.DMA
    n = WIN + 1
    return pl.pallas_call(
        main_kernel,
        out_shape=(
            jax.ShapeDtypeStruct((n, YN, 2, TOK, 128), BF16),
            jax.ShapeDtypeStruct((32, TOK), F32),
            jax.ShapeDtypeStruct((YN, 4, 16, 128), F32),
        ),
        in_specs=[sm] + [vm] * 7,
        out_specs=(pl.BlockSpec(memory_space=pl.ANY), vm, vm),
        scratch_shapes=[
            pltpu.VMEM((TPN, 32, TOK), F32),
            pltpu.SMEM((32, TOK), F32),
            pltpu.VMEM((16, 16, 128), F32),
            pltpu.VMEM((GROUP, 16, 128), F32),
            pltpu.VMEM((GROUP, 16, 128), F32),
            pltpu.VMEM((YN, 5, 16, 128), F32),
            pltpu.VMEM((YN, 5, 16, 128), F32),
            pltpu.VMEM((4, 5, 16, 128), F32),
            pltpu.VMEM((4, 5, 16, 128), F32),
            pltpu.VMEM((YN, 4, 16, 128), F32),
            pltpu.VMEM((YN, 4, 16, 128), F32),
            dma((2,)),
            dma(()),
        ]
        + [dma((2, n)) for _ in range(6)]
        + [dma((n,)) for _ in range(4)]
        + [dma((TPN,)), dma((TPN,))]
        + [dma((4,)) for _ in range(6)],
        compiler_params=pltpu.CompilerParams(collective_id=0, has_side_effects=True),
        name="gather_scan_exchange",
    )(lengths, k, v, x, w, dt, bias, a_log)


def final_kernel(len_ref, bc_ref, dt_ref, x_ref, bias_ref, alog_ref, skip_ref, inc_ref, out_ref, rate_s, step_s, u_s, state_s, y_s):
    base = lax.axis_index("seq") * TOK
    starts = starts_of(len_ref)
    rate_s[...] = (jnp.exp(alog_ref[...]) * (-LOG2E)).reshape(16, 16, 128)
    for n in range(16):
        state_s[n] = inc_ref[n // 4, n % 4]
    bias = bias_ref[...]
    skip = skip_ref[...]

    @pl.loop(0, TOK // GROUP)
    def _(g):
        fill_group(g, base, starts, dt_ref, x_ref, bias, step_s, u_s)

        def token(t, states):
            st = step_s[t]
            u = u_s[t]
            p = g * GROUP + t
            new = []
            acc = None
            for n in range(16):
                f = jnp.exp2(st * rate_s[n])
                s = f * states[n] + u * bc_ref[n, p]
                new.append(s)
                term = s * bc_ref[16 + n, p]
                acc = term if acc is None else acc + term
            y_s[t] = acc
            return tuple(new)

        states = lax.fori_loop(0, GROUP, token, tuple(state_s[n] for n in range(16)), unroll=2)
        for n in range(16):
            state_s[n] = states[n]
        rows = pl.ds(pl.multiple_of(g * GROUP, GROUP), GROUP)
        x = x_ref[rows, :].astype(F32)
        out_ref[rows, :] = (y_s[...].reshape(GROUP, 2048) + skip * x).astype(BF16)


def final_pass(lengths, bc, dt, x, bias, a_log, skip, inc):
    vm = pl.BlockSpec(memory_space=pltpu.VMEM)
    sm = pl.BlockSpec(memory_space=pltpu.SMEM)
    return pl.pallas_call(
        final_kernel,
        out_shape=jax.ShapeDtypeStruct(x.shape, BF16),
        in_specs=[sm, sm] + [vm] * 6,
        out_specs=vm,
        scratch_shapes=[
            pltpu.VMEM((16, 16, 128), F32),
            pltpu.VMEM((GROUP, 16, 128), F32),
            pltpu.VMEM((GROUP, 16, 128), F32),
            pltpu.VMEM((16, 16, 128), F32),
            pltpu.VMEM((GROUP, 16, 128), F32),
        ],
        name="scan_final",
    )(lengths, bc, dt, x, bias, a_log, skip, inc)


ROWS = 256
PLANE = YN * TOK


def attend_kernel(len_ref, idx_ref, num_ref, q_ref, win_ref, res_ref, table_ref, ctx_ref, st_ref):
    seq = lax.axis_index("seq")
    z = seq // YN
    base = seq * TOK
    starts = starts_of(len_ref)
    first_start = jnp.int32(0)
    for r in range(1, 4):
        first_start = jnp.where(starts[r] <= base, starts[r], first_start)
    planes = z - first_start // PLANE + 1
    scale = LOG2E / 128.0**0.5

    @pl.loop(0, 1024 // ROWS)
    def _(rt):
        rows = pl.ds(pl.multiple_of(rt * ROWS, ROWS), ROWS)
        q = q_ref[rows, :]
        pos = base + rt * (ROWS // 8) + lax.broadcasted_iota(jnp.int32, (ROWS, 1), 0) // 8
        start = jnp.zeros((ROWS, 1), jnp.int32)
        for r in range(4):
            start = jnp.where(pos >= starts[r], starts[r], start)

        def step(dz, carry):
            m, l, acc = carry
            k = win_ref[dz, :, 0].reshape(PLANE, 128)
            v = win_ref[dz, :, 1].reshape(PLANE, 128)
            s = lax.dot_general(q, k, (((1,), (1,)), ((), ())), preferred_element_type=F32)
            key_pos = (z - dz) * PLANE + lax.broadcasted_iota(jnp.int32, (1, PLANE), 1)
            ok = (key_pos <= pos) & (key_pos >= start)
            s = jnp.where(ok, s, NEG_FILL)
            m_new = jnp.maximum(m, jnp.max(s, axis=1, keepdims=True))
            e = jnp.exp2((s - m_new) * scale)
            fix = jnp.exp2((m - m_new) * scale)
            l = l * fix + jnp.sum(e, axis=1, keepdims=True)
            acc = acc * fix + jnp.dot(e.astype(BF16), v, preferred_element_type=F32)
            return m_new, l, acc

        init = (
            jnp.full((ROWS, 1), NEG_FILL, F32),
            jnp.zeros((ROWS, 1), F32),
            jnp.zeros((ROWS, 128), F32),
        )
        m, l, acc = lax.fori_loop(0, planes, step, init)
        ctx_ref[rows, :] = (acc / l).astype(BF16)

    tpos = base + lax.broadcasted_iota(jnp.int32, (TOK, 1), 0)
    add = jnp.zeros((TOK, 1024), F32)
    table = table_ref[...].astype(F32)
    for r in range(4):
        vec = jnp.zeros((1, 1024), F32)
        for i in range(7):
            vec = jnp.where(idx_ref[r] == i, table[i : i + 1], vec)
        add = jnp.where(tpos >= starts[r], vec * (num_ref[r].astype(F32) * 0.25), add)
    st_ref[...] = (res_ref[...].astype(F32) + add).astype(BF16)


def attend(lengths, index, num, q, win, residual, table):
    vm = pl.BlockSpec(memory_space=pltpu.VMEM)
    sm = pl.BlockSpec(memory_space=pltpu.SMEM)
    return pl.pallas_call(
        attend_kernel,
        out_shape=(jax.ShapeDtypeStruct(q.shape, BF16), jax.ShapeDtypeStruct(residual.shape, BF16)),
        in_specs=[sm, sm, sm, vm, vm, vm, vm],
        out_specs=(vm, vm),
        name="attend_steer",
    )(lengths, index, num, q, win, residual, table)


def shards(residual, steer_table, steer_index, steer_num, lengths, queries, keys, values, inner_x, dt_raw, dt_bias, a_log, skip_gain, bc_weight):
    bias = dt_bias[None, :]
    k = keys.reshape(TOK, 128)
    v = values.reshape(TOK, 128)
    win, bc, inc = main_pass(lengths, k, v, inner_x, bc_weight, dt_raw, bias, a_log)
    ctx, steered = attend(lengths, steer_index, steer_num, queries.reshape(1024, 128), win, residual, steer_table)
    mixed = final_pass(lengths, bc, dt_raw, inner_x, bias, a_log, skip_gain[None, :], inc)
    return steered, ctx.reshape(queries.shape), mixed


def solution(mesh):
    return jax.shard_map(
        shards,
        mesh=mesh,
        in_specs=(
            P("seq", "tp"),
            P(None, "tp"),
            P(),
            P(),
            P(),
            P("seq", "tp", None),
            P("seq", "tp", None),
            P("seq", "tp", None),
            P("seq", "tp"),
            P("seq", "tp"),
            P("tp"),
            P(None, "tp"),
            P("tp"),
            P(None, "tp"),
        ),
        out_specs=(P("seq", "tp"), P("seq", "tp", None), P("seq", "tp")),
        check_vma=False,
    )
```

time: 136 us -> 78.1 us (0.57)
  the two profiles are of different devices: /device:TPU:8 before, /device:TPU:264 now
where the time goes in v2:
time: 78.1 us; the launch traced here: 77.9 us
  Pallas kernels  77.3 us (99%)
    pallas_call x1, Pallas kernels, main_pass(): pl.pallas_call(main_kernel, out_shape=(jax.ShapeDtypeStruct((n, YN, 2, TO...  49.1 us
    pallas_call x1, Pallas kernels, attend(): pl.pallas_call(attend_kernel, out_shape=(jax.ShapeDtypeStruct(q.shape, BF...  18.7 us
    pallas_call x1, Pallas kernels, final_pass(): pl.pallas_call(final_kernel, out_shape=jax.ShapeDtypeStruct(x.shape, BF16...  9.53 us

profile of v2, /device:TPU:264, one launch (start us, length us, event | category | flops | bytes accessed | tf_op | source)
XLA Modules:
  0.0 77.9 jit_solution(11839065841235854224)
XLA Ops:
  0.6 49.1 %gather_scan_exchange.1 = (bf16[9,4,2,128,128]{4,3,2,1,0:T(8,128)(2,1)}, f32[32,128]{1,0:T(8,128)}, f32[4,4,16,128]{3,2,1,0:T(8,128)}) custom-call(s32[4]{0:T(128)} %len_ref.5, bf16[128,128]{1,0:T(8,128)(2,1)} %bitcast.9, bf16[128,128]{1,0:T(8,128)(2,1)} %bitcast.10, bf16[128,2048]{1,0:T(8,128)(2,1)} %x_ref.3, bf16[32,2048]{1,0:T(8,128)(2,1)} %w_ref.1, ...), custom_call_target="tpu_custom_call" | custom-call | tf_op jit(solution)/shard_map/gather_scan_exchange/pallas_call | solution.py:255
  49.7 18.7 %attend_steer.1 = (bf16[1024,128]{1,0:T(8,128)(2,1)}, bf16[128,1024]{1,0:T(8,128)(2,1)}) custom-call(s32[4]{0:T(128)} %len_ref.5, s32[4]{0:T(128)} %idx_ref.1, s32[4]{0:T(128)} %num_ref.1, bf16[1024,128]{1,0:T(8,128)(2,1)} %bitcast.6, bf16[9,4,2,128,128]{4,3,2,1,0:T(8,128)(2,1)} %get-tuple-element.8.win_ref, bf16[128,1024]{1,0:T(8,128)(2,1)} %res_ref.1, ...), custom_call_target="tpu_custom_call" | custom-call | tf_op jit(solution)/shard_map/attend_steer/pallas_call | solution.py:404
  68.4 9.5 %scan_final.1 = bf16[128,2048]{1,0:T(8,128)(2,1)} custom-call(s32[4]{0:T(128)} %len_ref.5, f32[32,128]{1,0:T(8,128)} %get-tuple-element.11.bc_ref, bf16[128,2048]{1,0:T(8,128)(2,1)} %dt_ref.3, bf16[128,2048]{1,0:T(8,128)(2,1)} %x_ref.3, f32[1,2048]{1,0:T(1,128)} %bitcast.8, f32[16,2048]{1,0:T(8,128)} %alog_ref.3, f32[1,2048]{1,0:T(1,128)} %bitcast.11, ...), custom_call_target="tpu_custom_call" | custom-call | tf_op jit(solution)/shard_map/scan_final/pallas_call | solution.py:327

commit v3 on v2

v3 whole, which is shorter than its diff:
```python
import functools
import jax
import jax.numpy as jnp
from jax import lax
from jax.experimental import pallas as pl
from jax.experimental.pallas import tpu as pltpu
from jax.sharding import PartitionSpec as P

LOG2E = 1.4426950408889634
NEG_FILL = -1e30
RESET = 1e30
YN = 4
ZN = 16
SEQ = YN * ZN
TPN = 8
WIN = 8
TOK = 128
ROWS = 256
PLANE = YN * TOK
GROUP = 16
MESH = pl.DeviceIdType.MESH
F32 = jnp.float32
BF16 = jnp.bfloat16


def starts_of(len_ref):
    s1 = len_ref[0]
    s2 = s1 + len_ref[1]
    s3 = s2 + len_ref[2]
    return (jnp.int32(0), s1, s2, s3)


def log1p_exp(v):
    return jnp.maximum(v, 0.0) + jnp.log1p(jnp.exp(-jnp.abs(v)))


def fill_group(g, base, starts, dt_ref, x_ref, bias, step_s, u_s):
    rows = pl.ds(pl.multiple_of(g * GROUP, GROUP), GROUP)
    raw = dt_ref[rows, :].astype(F32)
    x = x_ref[rows, :].astype(F32)
    step = log1p_exp(raw + bias)
    pos = base + g * GROUP + lax.broadcasted_iota(jnp.int32, (GROUP, 1), 0)
    hit = (pos == starts[0]) | (pos == starts[1]) | (pos == starts[2]) | (pos == starts[3])
    u_s[pl.ds(g * GROUP, GROUP)] = (step * x).reshape(GROUP, 16, 128)
    step_s[...] = (step + jnp.where(hit, RESET, 0.0)).reshape(GROUP, 16, 128)


def main_kernel(
    len_ref, idx_ref, num_ref, k_ref, v_ref, x_ref, w_ref, dt_ref, bias_ref, alog_ref, skip_ref, q_ref, res_ref, table_ref,
    ctx_ref, st_ref, out_ref,
    win_ref, parts, bc_v, bc_s, rate_s, step_s, u_s, fac_s, msg, ych, zout, zin, outb, inc_s, y_s, start_s, m_s, l_s, acc_s,
    own_sem, bc_sem, zs, zr, rs, rr, ls, lr, ks, kr, vs, vr, bs, br, ps, pr, qs, qr, fs, fr,
):
    seq = lax.axis_index("seq")
    tp = lax.axis_index("tp")
    z = seq // YN
    y = lax.rem(seq, YN)
    left_y = lax.rem(y + YN - 1, YN)
    right_y = lax.rem(y + 1, YN)

    def zy(dz, dy):
        return lax.rem(z + dz, ZN) * YN + lax.rem(y + dy, YN)

    up = zy(1, 0)
    right = zy(0, 1)
    left = zy(0, YN - 1)

    barrier = pltpu.get_barrier_semaphore()
    for dz in (1, 2, 4, ZN - 1, ZN - 2, ZN - 4):
        pl.semaphore_signal(barrier, inc=1, device_id=(zy(dz, 0), tp), device_id_type=MESH)
    for dy in range(1, YN):
        pl.semaphore_signal(barrier, inc=1, device_id=(zy(0, dy), tp), device_id_type=MESH)
    for off in range(1, TPN):
        pl.semaphore_signal(barrier, inc=1, device_id=(seq, lax.rem(tp + off, TPN)), device_id_type=MESH)
    pl.semaphore_wait(barrier, 6 + YN - 1 + TPN - 1)

    def remote(src, dst, ssem, rsem, peer):
        return pltpu.make_async_remote_copy(
            src_ref=src, dst_ref=dst, send_sem=ssem, recv_sem=rsem, device_id=(peer, tp), device_id_type=MESH
        )

    def block(s, h):
        return (k_ref, v_ref)[h] if s == 0 else win_ref.at[s, y, h]

    def z_copy(s, h):
        return remote(block(s - 1, h), win_ref.at[s, y, h], zs.at[h, s], zr.at[h, s], up)

    def right_copy(s, h):
        return remote(block(s, h), win_ref.at[s, y, h], rs.at[h, s], rr.at[h, s], right)

    def left_copy(s, h):
        return remote(block(s, h), win_ref.at[s, y, h], ls.at[h, s], lr.at[h, s], left)

    def k_copy(s):
        return remote(win_ref.at[s, left_y, 0], win_ref.at[s, left_y, 0], ks.at[s], kr.at[s], right)

    def v_copy(s):
        return remote(win_ref.at[s, right_y, 1], win_ref.at[s, right_y, 1], vs.at[s], vr.at[s], left)

    def spread(s):
        right_copy(s - 1, 0).wait_recv()
        k_copy(s - 1).start()
        left_copy(s - 1, 1).wait_recv()
        v_copy(s - 1).start()

    def kv_step(s):
        for h in (0, 1):
            z_copy(s, h).wait_recv()
            if s < WIN:
                z_copy(s + 1, h).start()
            right_copy(s, h).start()
            left_copy(s, h).start()
        spread(s)

    own = [pltpu.make_async_copy((k_ref, v_ref)[h], win_ref.at[0, y, h], own_sem.at[h]) for h in (0, 1)]
    for h in (0, 1):
        z_copy(1, h).start()
    for h in (0, 1):
        right_copy(0, h).start()
        left_copy(0, h).start()
        own[h].start()

    parts[tp] = lax.dot_general(w_ref[...], x_ref[...], (((1,), (1,)), ((), ())), preferred_element_type=F32)

    def bc_copy(off):
        return pltpu.make_async_remote_copy(
            src_ref=parts.at[tp], dst_ref=parts.at[tp], send_sem=bs.at[off], recv_sem=br.at[off],
            device_id=(seq, lax.rem(tp + off, TPN)), device_id_type=MESH,
        )

    for off in range(1, TPN):
        bc_copy(off).start()

    rate_s[...] = (jnp.exp(alog_ref[...]) * (-LOG2E)).reshape(16, 16, 128)
    msg[...] = jnp.zeros_like(msg)
    bias = bias_ref[...]
    base = seq * TOK
    starts = starts_of(len_ref)
    scale = LOG2E / 128.0**0.5

    def ready(dz):
        right_copy(dz, 1).wait_recv()
        left_copy(dz, 0).wait_recv()
        k_copy(dz).wait_recv()
        v_copy(dz).wait_recv()

    def attend_plane(dz):
        ready(dz)

        @pl.when(z >= dz)
        def _():
            @pl.loop(0, 1024 // ROWS)
            def _(rt):
                rows = pl.ds(pl.multiple_of(rt * ROWS, ROWS), ROWS)
                key_pos = lax.broadcasted_iota(jnp.int32, (1, PLANE), 1)
                first = start_s[rows, :] - (z - dz) * PLANE
                kk = win_ref[dz, :, 0].reshape(PLANE, 128)
                vv = win_ref[dz, :, 1].reshape(PLANE, 128)
                sc = lax.dot_general(q_ref[rows, :], kk, (((1,), (1,)), ((), ())), preferred_element_type=F32)
                ok = key_pos >= first
                if dz == 0:
                    last = y * TOK + rt * (ROWS // 8) + lax.broadcasted_iota(jnp.int32, (ROWS, 1), 0) // 8
                    ok = ok & (key_pos <= last)
                sc = jnp.where(ok, sc, NEG_FILL)
                top = jnp.max(sc, axis=1, keepdims=True)
                if dz == 0:
                    e = jnp.exp2((sc - top) * scale)
                    l_s[rows, :] = jnp.sum(e, axis=1, keepdims=True)
                    acc_s[rows, :] = jnp.dot(e.astype(BF16), vv, preferred_element_type=F32)
                    m_s[rows, :] = top
                else:
                    old = m_s[rows, :]
                    top = jnp.maximum(old, top)
                    e = jnp.exp2((sc - top) * scale)
                    fix = jnp.exp2((old - top) * scale)
                    l_s[rows, :] = l_s[rows, :] * fix + jnp.sum(e, axis=1, keepdims=True)
                    acc_s[rows, :] = acc_s[rows, :] * fix + jnp.dot(e.astype(BF16), vv, preferred_element_type=F32)
                    m_s[rows, :] = top

    qpos = base + lax.broadcasted_iota(jnp.int32, (1024, 1), 0) // 8
    qstart = jnp.zeros((1024, 1), jnp.int32)
    for r in range(1, 4):
        qstart = jnp.where(qpos >= starts[r], starts[r], qstart)
    start_s[...] = qstart

    table = table_ref[...].astype(F32)
    tpos = base + lax.broadcasted_iota(jnp.int32, (TOK, 1), 0)
    add = jnp.zeros((TOK, 1024), F32)
    for r in range(4):
        vec = jnp.zeros((1, 1024), F32)
        for i in range(7):
            vec = jnp.where(idx_ref[r] == i, table[i : i + 1], vec)
        add = jnp.where(tpos >= starts[r], vec * (num_ref[r].astype(F32) * 0.25), add)
    st_ref[...] = (res_ref[...].astype(F32) + add).astype(BF16)

    kv_step(1)
    for off in range(1, TPN):
        bc_copy(off).wait_recv()
    total_bc = parts[0]
    for t in range(1, TPN):
        total_bc = total_bc + parts[t]
    bc_v[...] = total_bc
    to_smem = pltpu.make_async_copy(bc_v, bc_s, bc_sem)
    to_smem.start()
    to_smem.wait()

    def scan_groups(lo, hi):
        @pl.loop(lo, hi)
        def _(g):
            fill_group(g, base, starts, dt_ref, x_ref, bias, step_s, u_s)

            def token(t, carry):
                states, total = carry
                st = step_s[t]
                p = g * GROUP + t
                u = u_s[p]
                new = []
                for n in range(16):
                    f = jnp.exp2(st * rate_s[n])
                    fac_s[p, n] = f
                    new.append(f * states[n] + u * bc_s[n, p])
                return tuple(new), total + st

            init = (tuple(msg[n // 4, n % 4] for n in range(16)), msg[0, 4])
            states, total = lax.fori_loop(0, GROUP, token, init, unroll=2)
            for n in range(16):
                msg[n // 4, n % 4] = states[n]
            msg[0, 4] = total

    scan_groups(0, 3)
    kv_step(2)
    scan_groups(3, 6)
    kv_step(3)
    scan_groups(6, 8)
    total = msg[0, 4]
    for q in range(1, 4):
        msg[q, 4] = total

    def part_copy(d):
        return remote(msg.at[lax.rem(y + d, YN)], ych.at[y], ps.at[d], pr.at[d], zy(0, d))

    for d in (1, 3, 2):
        part_copy(d).start()
    ych[y] = msg[y]
    kv_step(4)
    for h in (0, 1):
        own[h].wait()
    attend_plane(0)
    attend_plane(1)
    for d in range(1, YN):
        part_copy(d).wait_recv()
    rate = rate_s[pl.ds(4 * y, 4)]
    acc = ych[0, 0:4]
    dec = ych[0, 4]
    for c in range(1, YN):
        acc = jnp.exp2(rate * ych[c, 4][None]) * acc + ych[c, 0:4]
        dec = dec + ych[c, 4]

    def z_round(j, d):
        return remote(zout.at[j], zin.at[j], qs.at[j], qr.at[j], zy(d, 0))

    for j, d in enumerate((1, 1, 2, 4)):
        zout[j, 0:4] = acc
        zout[j, 4] = dec
        z_round(j, d).start()
        kv_step(5 + j)
        for dz in ((), (2,), (3, 4), (5, 6))[j]:
            attend_plane(dz)
        z_round(j, d).wait_recv()
        here = (z >= d).astype(F32)
        got = zin[j, 0:4] * here
        got_dec = zin[j, 4] * here
        if j == 0:
            acc, dec = got, got_dec
        else:
            acc = acc + jnp.exp2(rate * dec[None]) * got
            dec = dec + got_dec

    for c in range(YN):
        outb[c] = acc
        if c < YN - 1:
            acc = jnp.exp2(rate * ych[c, 4][None]) * acc + ych[c, 0:4]

    def back_copy(d):
        return remote(outb.at[lax.rem(y + d, YN)], inc_s.at[y], fs.at[d], fr.at[d], zy(0, d))

    for d in (1, 3, 2):
        back_copy(d).start()
    inc_s[y] = outb[y]
    spread(WIN + 1)
    attend_plane(7)
    attend_plane(8)
    ctx_ref[...] = (acc_s[...] / l_s[...]).astype(BF16)
    for d in range(1, YN):
        back_copy(d).wait_recv()
    skip = skip_ref[...]

    @pl.loop(0, TOK // GROUP)
    def _(g):
        def token(t, states):
            p = g * GROUP + t
            u = u_s[p]
            new = []
            total = None
            for n in range(16):
                state = fac_s[p, n] * states[n] + u * bc_s[n, p]
                new.append(state)
                term = state * bc_s[16 + n, p]
                total = term if total is None else total + term
            y_s[t] = total
            return tuple(new)

        states = lax.fori_loop(0, GROUP, token, tuple(inc_s[n // 4, n % 4] for n in range(16)), unroll=2)
        for n in range(16):
            inc_s[n // 4, n % 4] = states[n]
        rows = pl.ds(pl.multiple_of(g * GROUP, GROUP), GROUP)
        x = x_ref[rows, :].astype(F32)
        out_ref[rows, :] = (y_s[...].reshape(GROUP, 2048) + skip * x).astype(BF16)

    for off in range(1, TPN):
        bc_copy(off).wait_send()
    for d in range(1, YN):
        part_copy(d).wait_send()
        back_copy(d).wait_send()
    for j, d in enumerate((1, 1, 2, 4)):
        z_round(j, d).wait_send()
    for s in range(WIN + 1):
        for h in (0, 1):
            if s > 0:
                z_copy(s, h).wait_send()
            right_copy(s, h).wait_send()
            left_copy(s, h).wait_send()
        k_copy(s).wait_send()
        v_copy(s).wait_send()


def main_pass(*args):
    vm = pl.BlockSpec(memory_space=pltpu.VMEM)
    sm = pl.BlockSpec(memory_space=pltpu.SMEM)
    dma = pltpu.SemaphoreType.DMA
    n = WIN + 1
    return pl.pallas_call(
        main_kernel,
        out_shape=(
            jax.ShapeDtypeStruct((1024, 128), BF16),
            jax.ShapeDtypeStruct((TOK, 1024), BF16),
            jax.ShapeDtypeStruct((TOK, 2048), BF16),
        ),
        in_specs=[sm] * 3 + [vm] * 11,
        out_specs=(vm, vm, vm),
        scratch_shapes=[
            pltpu.VMEM((n, YN, 2, TOK, 128), BF16),
            pltpu.VMEM((TPN, 32, TOK), F32),
            pltpu.VMEM((32, TOK), F32),
            pltpu.SMEM((32, TOK), F32),
            pltpu.VMEM((16, 16, 128), F32),
            pltpu.VMEM((GROUP, 16, 128), F32),
            pltpu.VMEM((TOK, 16, 128), F32),
            pltpu.VMEM((TOK, 16, 16, 128), F32),
            pltpu.VMEM((YN, 5, 16, 128), F32),
            pltpu.VMEM((YN, 5, 16, 128), F32),
            pltpu.VMEM((4, 5, 16, 128), F32),
            pltpu.VMEM((4, 5, 16, 128), F32),
            pltpu.VMEM((YN, 4, 16, 128), F32),
            pltpu.VMEM((YN, 4, 16, 128), F32),
            pltpu.VMEM((GROUP, 16, 128), F32),
            pltpu.VMEM((1024, 1), jnp.int32),
            pltpu.VMEM((1024, 1), F32),
            pltpu.VMEM((1024, 1), F32),
            pltpu.VMEM((1024, 128), F32),
            dma((2,)),
            dma(()),
        ]
        + [dma((2, n)) for _ in range(6)]
        + [dma((n,)) for _ in range(4)]
        + [dma((TPN,)), dma((TPN,))]
        + [dma((4,)) for _ in range(6)],
        compiler_params=pltpu.CompilerParams(collective_id=0, has_side_effects=True),
        name="layer",
    )(*args)


def shards(residual, steer_table, steer_index, steer_num, lengths, queries, keys, values, inner_x, dt_raw, dt_bias, a_log, skip_gain, bc_weight):
    ctx, steered, mixed = main_pass(
        lengths,
        steer_index,
        steer_num,
        keys.reshape(TOK, 128),
        values.reshape(TOK, 128),
        inner_x,
        bc_weight,
        dt_raw,
        dt_bias[None, :],
        a_log,
        skip_gain[None, :],
        queries.reshape(1024, 128),
        residual,
        steer_table,
    )
    return steered, ctx.reshape(queries.shape), mixed


def solution(mesh):
    return jax.shard_map(
        shards,
        mesh=mesh,
        in_specs=(
            P("seq", "tp"),
            P(None, "tp"),
            P(),
            P(),
            P(),
            P("seq", "tp", None),
            P("seq", "tp", None),
            P("seq", "tp", None),
            P("seq", "tp"),
            P("seq", "tp"),
            P("tp"),
            P(None, "tp"),
            P("tp"),
            P(None, "tp"),
        ),
        out_specs=(P("seq", "tp"), P("seq", "tp", None), P("seq", "tp")),
        check_vma=False,
    )
```

time: 78.1 us -> 67.9 us (0.87)
  the two profiles are of different devices: /device:TPU:264 before, /device:TPU:32 now
where the time goes in v3:
time: 67.9 us; the launch traced here: 67.7 us
  Pallas kernels  63.8 us (94%)
  local copies, waits for them, and re-layouts  3.24 us (5%)
    pallas_call x1, Pallas kernels, main_pass(): pl.pallas_call(main_kernel, out_shape=(jax.ShapeDtypeStruct((1024, 128),...  63.8 us
    unnamed x7, local copies, waits for them, and re-layouts  3.24 us

profile of v3, /device:TPU:32, one launch (start us, length us, event | category | flops | bytes accessed | tf_op | source)
XLA Modules:
  0.0 67.7 jit_solution(11772912444791030131)
XLA Ops:
  0.6 63.8 %layer.1 = (bf16[1024,128]{1,0:T(8,128)(2,1)}, bf16[128,1024]{1,0:T(8,128)(2,1)}, bf16[128,2048]{1,0:T(8,128)(2,1)}) custom-call(s32[4]{0:T(128)} %len_ref.1, s32[4]{0:T(128)} %idx_ref.1, s32[4]{0:T(128)} %num_ref.1, bf16[128,128]{1,0:T(8,128)(2,1)} %bitcast.8, bf16[128,128]{1,0:T(8,128)(2,1)} %bitcast.9, bf16[128,2048]{1,0:T(8,128)(2,1)} %x_ref.1, ...), custom_call_target="tpu_custom_call" | custom-call | tf_op jit(solution)/shard_map/layer/pallas_call | solution.py:342
  64.4 0.0 copy-start.1
  64.5 0.0 copy-start
  64.5 1.7 %copy.20 = bf16[128,1024]{1,0:T(8,128)(2,1)} copy(bf16[128,1024]{1,0:T(8,128)(2,1)} %get-tuple-element.12) | data formatting | bytes 524288
  66.2 0.0 copy-done.1
  66.2 0.7 %copy.21 = bf16[128,8,128]{2,1,0:T(8,128)(2,1)} copy(bf16[128,8,128]{2,1,0:T(8,128)(2,1)S(1)} %bitcast.6) | data formatting | bytes 524288
  66.9 0.0 copy-done
  66.9 0.8 %copy.22 = bf16[128,2048]{1,0:T(8,128)(2,1)} copy(bf16[128,2048]{1,0:T(8,128)(2,1)S(1)} %copy-done) | data formatting | bytes 1048576
Async XLA Ops:
  64.4 1.8 %copy-start.1 = (bf16[1024,128]{1,0:T(8,128)(2,1)S(1)}, bf16[1024,128]{1,0:T(8,128)(2,1)}, u32[]{:S(2)}) copy-start(bf16[1024,128]{1,0:T(8,128)(2,1)} %get-tuple-element.7) | copy-start | bytes 786436
  64.5 2.5 %copy-start = (bf16[128,2048]{1,0:T(8,128)(2,1)S(1)}, bf16[128,2048]{1,0:T(8,128)(2,1)}, u32[]{:S(2)}) copy-start(bf16[128,2048]{1,0:T(8,128)(2,1)} %get-tuple-element.14) | copy-start | bytes 1572868

commit v4 on v3

--- a/solution.py
+++ b/solution.py
@@ -46,9 +46,9 @@
 
 
 def main_kernel(
-    len_ref, idx_ref, num_ref, k_ref, v_ref, x_ref, w_ref, dt_ref, bias_ref, alog_ref, skip_ref, q_ref, res_ref, table_ref,
-    ctx_ref, st_ref, out_ref,
-    win_ref, parts, bc_v, bc_s, rate_s, step_s, u_s, fac_s, msg, ych, zout, zin, outb, inc_s, y_s, start_s, m_s, l_s, acc_s,
+    len_ref, k_ref, v_ref, x_ref, w_ref, dt_ref, bias_ref, alog_ref, skip_ref, q_ref,
+    ctx_ref, out_ref,
+    win_ref, parts, bc_v, bc_s, rate_s, step_s, u_s, fac_s, msg, ych, zout, zin, outb, inc_s, y_s, start_s, m_s, l_s, acc_s, qt_s, vt_s,
     own_sem, bc_sem, zs, zr, rs, rr, ls, lr, ks, kr, vs, vr, bs, br, ps, pr, qs, qr, fs, fr,
 ):
     seq = lax.axis_index("seq")
@@ -149,49 +149,41 @@
 
         @pl.when(z >= dz)
         def _():
+            vt_s[...] = win_ref[dz, :, 1].reshape(PLANE, 128).astype(F32).T.astype(BF16)
+
             @pl.loop(0, 1024 // ROWS)
             def _(rt):
-                rows = pl.ds(pl.multiple_of(rt * ROWS, ROWS), ROWS)
-                key_pos = lax.broadcasted_iota(jnp.int32, (1, PLANE), 1)
-                first = start_s[rows, :] - (z - dz) * PLANE
+                cols = pl.ds(pl.multiple_of(rt * ROWS, ROWS), ROWS)
                 kk = win_ref[dz, :, 0].reshape(PLANE, 128)
-                vv = win_ref[dz, :, 1].reshape(PLANE, 128)
-                sc = lax.dot_general(q_ref[rows, :], kk, (((1,), (1,)), ((), ())), preferred_element_type=F32)
+                key_pos = lax.broadcasted_iota(jnp.int32, (PLANE, ROWS), 0)
+                first = start_s[:, cols] - (z - dz) * PLANE
+                sc = jnp.dot(kk, qt_s[:, cols], preferred_element_type=F32)
                 ok = key_pos >= first
                 if dz == 0:
-                    last = y * TOK + rt * (ROWS // 8) + lax.broadcasted_iota(jnp.int32, (ROWS, 1), 0) // 8
+                    last = y * TOK + rt * (ROWS // 8) + lax.broadcasted_iota(jnp.int32, (1, ROWS), 1) // 8
                     ok = ok & (key_pos <= last)
                 sc = jnp.where(ok, sc, NEG_FILL)
-                top = jnp.max(sc, axis=1, keepdims=True)
-                if dz == 0:
-                    e = jnp.exp2((sc - top) * scale)
-                    l_s[rows, :] = jnp.sum(e, axis=1, keepdims=True)
-                    acc_s[rows, :] = jnp.dot(e.astype(BF16), vv, preferred_element_type=F32)
-                    m_s[rows, :] = top
-                else:
-                    old = m_s[rows, :]
+                top = jnp.max(sc, axis=0, keepdims=True)
+                if dz > 0:
+                    old = m_s[:, cols]
                     top = jnp.maximum(old, top)
-                    e = jnp.exp2((sc - top) * scale)
+                e = jnp.exp2((sc - top) * scale)
+                total = jnp.sum(e, axis=0, keepdims=True)
+                prod = jnp.dot(vt_s[...], e.astype(BF16), preferred_element_type=F32)
+                if dz > 0:
                     fix = jnp.exp2((old - top) * scale)
-                    l_s[rows, :] = l_s[rows, :] * fix + jnp.sum(e, axis=1, keepdims=True)
-                    acc_s[rows, :] = acc_s[rows, :] * fix + jnp.dot(e.astype(BF16), vv, preferred_element_type=F32)
-                    m_s[rows, :] = top
-
-    qpos = base + lax.broadcasted_iota(jnp.int32, (1024, 1), 0) // 8
-    qstart = jnp.zeros((1024, 1), jnp.int32)
+                    total = l_s[:, cols] * fix + total
+                    prod = acc_s[:, cols] * fix + prod
+                m_s[:, cols] = top
+                l_s[:, cols] = total
+                acc_s[:, cols] = prod
+
+    qpos = base + lax.broadcasted_iota(jnp.int32, (1, 1024), 1) // 8
+    qstart = jnp.zeros((1, 1024), jnp.int32)
     for r in range(1, 4):
         qstart = jnp.where(qpos >= starts[r], starts[r], qstart)
     start_s[...] = qstart
-
-    table = table_ref[...].astype(F32)
-    tpos = base + lax.broadcasted_iota(jnp.int32, (TOK, 1), 0)
-    add = jnp.zeros((TOK, 1024), F32)
-    for r in range(4):
-        vec = jnp.zeros((1, 1024), F32)
-        for i in range(7):
-            vec = jnp.where(idx_ref[r] == i, table[i : i + 1], vec)
-        add = jnp.where(tpos >= starts[r], vec * (num_ref[r].astype(F32) * 0.25), add)
-    st_ref[...] = (res_ref[...].astype(F32) + add).astype(BF16)
+    qt_s[...] = q_ref[...].astype(F32).T.astype(BF16)
 
     kv_step(1)
     for off in range(1, TPN):
@@ -222,7 +214,7 @@
                 return tuple(new), total + st
 
             init = (tuple(msg[n // 4, n % 4] for n in range(16)), msg[0, 4])
-            states, total = lax.fori_loop(0, GROUP, token, init, unroll=2)
+            states, total = lax.fori_loop(0, GROUP, token, init, unroll=4)
             for n in range(16):
                 msg[n // 4, n % 4] = states[n]
             msg[0, 4] = total
@@ -266,6 +258,9 @@
         kv_step(5 + j)
         for dz in ((), (2,), (3, 4), (5, 6))[j]:
             attend_plane(dz)
+        if j == 3:
+            spread(WIN + 1)
+            attend_plane(7)
         z_round(j, d).wait_recv()
         here = (z >= d).astype(F32)
         got = zin[j, 0:4] * here
@@ -287,10 +282,8 @@
     for d in (1, 3, 2):
         back_copy(d).start()
     inc_s[y] = outb[y]
-    spread(WIN + 1)
-    attend_plane(7)
     attend_plane(8)
-    ctx_ref[...] = (acc_s[...] / l_s[...]).astype(BF16)
+    ctx_ref[...] = (acc_s[...] / l_s[...]).T.astype(BF16)
     for d in range(1, YN):
         back_copy(d).wait_recv()
     skip = skip_ref[...]
@@ -310,7 +303,7 @@
             y_s[t] = total
             return tuple(new)
 
-        states = lax.fori_loop(0, GROUP, token, tuple(inc_s[n // 4, n % 4] for n in range(16)), unroll=2)
+        states = lax.fori_loop(0, GROUP, token, tuple(inc_s[n // 4, n % 4] for n in range(16)), unroll=4)
         for n in range(16):
             inc_s[n // 4, n % 4] = states[n]
         rows = pl.ds(pl.multiple_of(g * GROUP, GROUP), GROUP)
@@ -343,11 +336,10 @@
         main_kernel,
         out_shape=(
             jax.ShapeDtypeStruct((1024, 128), BF16),
-            jax.ShapeDtypeStruct((TOK, 1024), BF16),
             jax.ShapeDtypeStruct((TOK, 2048), BF16),
         ),
-        in_specs=[sm] * 3 + [vm] * 11,
-        out_specs=(vm, vm, vm),
+        in_specs=[sm] + [vm] * 9,
+        out_specs=(vm, vm),
         scratch_shapes=[
             pltpu.VMEM((n, YN, 2, TOK, 128), BF16),
             pltpu.VMEM((TPN, 32, TOK), F32),
@@ -364,10 +356,12 @@
             pltpu.VMEM((YN, 4, 16, 128), F32),
             pltpu.VMEM((YN, 4, 16, 128), F32),
             pltpu.VMEM((GROUP, 16, 128), F32),
-            pltpu.VMEM((1024, 1), jnp.int32),
-            pltpu.VMEM((1024, 1), F32),
-            pltpu.VMEM((1024, 1), F32),
-            pltpu.VMEM((1024, 128), F32),
+            pltpu.VMEM((1, 1024), jnp.int32),
+            pltpu.VMEM((1, 1024), F32),
+            pltpu.VMEM((1, 1024), F32),
+            pltpu.VMEM((128, 1024), F32),
+            pltpu.VMEM((128, 1024), BF16),
+            pltpu.VMEM((128, PLANE), BF16),
             dma((2,)),
             dma(()),
         ]
@@ -380,11 +374,37 @@
     )(*args)
 
 
+def finish_kernel(len_ref, idx_ref, num_ref, ctx_ref, mix_ref, res_ref, table_ref, ctx_out, mix_out, st_out):
+    base = lax.axis_index("seq") * TOK
+    starts = starts_of(len_ref)
+    ctx_out[...] = ctx_ref[...]
+    mix_out[...] = mix_ref[...]
+    table = table_ref[...].astype(F32)
+    tpos = base + lax.broadcasted_iota(jnp.int32, (TOK, 1), 0)
+    add = jnp.zeros((TOK, 1024), F32)
+    for r in range(4):
+        vec = jnp.zeros((1, 1024), F32)
+        for i in range(7):
+            vec = jnp.where(idx_ref[r] == i, table[i : i + 1], vec)
+        add = jnp.where(tpos >= starts[r], vec * (num_ref[r].astype(F32) * 0.25), add)
+    st_out[...] = (res_ref[...].astype(F32) + add).astype(BF16)
+
+
+def finish(lengths, index, num, ctx, mixed, residual, table):
+    vm = pl.BlockSpec(memory_space=pltpu.VMEM)
+    sm = pl.BlockSpec(memory_space=pltpu.SMEM)
+    return pl.pallas_call(
+        finish_kernel,
+        out_shape=tuple(jax.ShapeDtypeStruct(v.shape, BF16) for v in (ctx, mixed, residual)),
+        in_specs=[sm] * 3 + [vm] * 4,
+        out_specs=(vm, vm, vm),
+        name="steer_finish",
+    )(lengths, index, num, ctx, mixed, residual, table)
+
+
 def shards(residual, steer_table, steer_index, steer_num, lengths, queries, keys, values, inner_x, dt_raw, dt_bias, a_log, skip_gain, bc_weight):
-    ctx, steered, mixed = main_pass(
+    ctx, mixed = main_pass(
         lengths,
-        steer_index,
-        steer_num,
         keys.reshape(TOK, 128),
         values.reshape(TOK, 128),
         inner_x,
@@ -394,9 +414,8 @@
         a_log,
         skip_gain[None, :],
         queries.reshape(1024, 128),
-        residual,
-        steer_table,
     )
+    ctx, mixed, steered = finish(lengths, steer_index, steer_num, ctx, mixed, residual, steer_table)
     return steered, ctx.reshape(queries.shape), mixed
 
 

time: 67.9 us -> 65.9 us (0.971)
  the two profiles are of different devices: /device:TPU:32 before, /device:TPU:4 now
where the time goes in v4:
time: 65.9 us; the launch traced here: 65.7 us
  Pallas kernels  65.1 us (99%)
    pallas_call x1, Pallas kernels, main_pass(): pl.pallas_call(main_kernel, out_shape=(jax.ShapeDtypeStruct((1024, 128),...  62.9 us
    pallas_call x1, Pallas kernels, finish(): pl.pallas_call(finish_kernel, out_shape=tuple((jax.ShapeDtypeStruct(v.sha...  2.22 us

profile of v4, /device:TPU:4, one launch (start us, length us, event | category | flops | bytes accessed | tf_op | source)
XLA Modules:
  0.0 65.7 jit_solution(3225513094678471971)
XLA Ops:
  0.6 62.9 %layer.1 = (bf16[1024,128]{1,0:T(8,128)(2,1)}, bf16[128,2048]{1,0:T(8,128)(2,1)}) custom-call(s32[4]{0:T(128)} %len_ref.3, bf16[128,128]{1,0:T(8,128)(2,1)} %bitcast.7, bf16[128,128]{1,0:T(8,128)(2,1)} %bitcast.8, bf16[128,2048]{1,0:T(8,128)(2,1)} %x_ref.1, bf16[32,2048]{1,0:T(8,128)(2,1)} %w_ref.1, bf16[128,2048]{1,0:T(8,128)(2,1)} %dt_ref.1, ...), custom_call_target="tpu_custom_call" | custom-call | tf_op jit(solution)/shard_map/layer/pallas_call | solution.py:335
  63.5 2.2 %steer_finish.1 = (bf16[1024,128]{1,0:T(8,128)(2,1)}, bf16[128,2048]{1,0:T(8,128)(2,1)}, bf16[128,1024]{1,0:T(8,128)(2,1)}) custom-call(s32[4]{0:T(128)} %len_ref.3, s32[4]{0:T(128)} %idx_ref.1, s32[4]{0:T(128)} %num_ref.1, bf16[1024,128]{1,0:T(8,128)(2,1)} %get-tuple-element.8.ctx_ref, bf16[128,2048]{1,0:T(8,128)(2,1)} %get-tuple-element.9.mix_ref, ...), custom_call_target="tpu_custom_call" | custom-call | tf_op jit(solution)/shard_map/steer_finish/pallas_call | solution.py:396

commit v5 on v4

--- a/solution.py
+++ b/solution.py
@@ -42,13 +42,13 @@
     pos = base + g * GROUP + lax.broadcasted_iota(jnp.int32, (GROUP, 1), 0)
     hit = (pos == starts[0]) | (pos == starts[1]) | (pos == starts[2]) | (pos == starts[3])
     u_s[pl.ds(g * GROUP, GROUP)] = (step * x).reshape(GROUP, 16, 128)
-    step_s[...] = (step + jnp.where(hit, RESET, 0.0)).reshape(GROUP, 16, 128)
+    step_s[pl.ds(g * GROUP, GROUP)] = (step + jnp.where(hit, RESET, 0.0)).reshape(GROUP, 16, 128)
 
 
 def main_kernel(
     len_ref, k_ref, v_ref, x_ref, w_ref, dt_ref, bias_ref, alog_ref, skip_ref, q_ref,
     ctx_ref, out_ref,
-    win_ref, parts, bc_v, bc_s, rate_s, step_s, u_s, fac_s, msg, ych, zout, zin, outb, inc_s, y_s, start_s, m_s, l_s, acc_s, qt_s, vt_s,
+    win_ref, parts, bc_v, bc_s, rate_s, step_s, u_s, fac_s, msg, ych, zout, zin, outb, inc_s, y_s, start_s, m_s, l_s, acc_s, qt_s, vt_s, far_out, far_in,
     own_sem, bc_sem, zs, zr, rs, rr, ls, lr, ks, kr, vs, vr, bs, br, ps, pr, qs, qr, fs, fr,
 ):
     seq = lax.axis_index("seq")
@@ -185,7 +185,21 @@
     start_s[...] = qstart
     qt_s[...] = q_ref[...].astype(F32).T.astype(BF16)
 
+    def factors(p, c):
+        st = step_s[p]
+        for n in range(16):
+            fac_s[p, n] = jnp.exp2(st * rate_s[n])
+        return c
+
+    def prepare(lo, hi):
+        @pl.loop(lo, hi)
+        def _(g):
+            fill_group(g, base, starts, dt_ref, x_ref, bias, step_s, u_s)
+            lax.fori_loop(g * GROUP, g * GROUP + GROUP, factors, 0)
+
+    prepare(0, 5)
     kv_step(1)
+    prepare(5, 8)
     for off in range(1, TPN):
         bc_copy(off).wait_recv()
     total_bc = parts[0]
@@ -199,18 +213,14 @@
     def scan_groups(lo, hi):
         @pl.loop(lo, hi)
         def _(g):
-            fill_group(g, base, starts, dt_ref, x_ref, bias, step_s, u_s)
-
             def token(t, carry):
                 states, total = carry
-                st = step_s[t]
                 p = g * GROUP + t
+                st = step_s[p]
                 u = u_s[p]
                 new = []
                 for n in range(16):
-                    f = jnp.exp2(st * rate_s[n])
-                    fac_s[p, n] = f
-                    new.append(f * states[n] + u * bc_s[n, p])
+                    new.append(fac_s[p, n] * states[n] + u * bc_s[n, p])
                 return tuple(new), total + st
 
             init = (tuple(msg[n // 4, n % 4] for n in range(16)), msg[0, 4])
@@ -249,11 +259,16 @@
         dec = dec + ych[c, 4]
 
     def z_round(j, d):
+        if j == 3:
+            return remote(far_out, far_in, qs.at[j], qr.at[j], zy(d, 0))
         return remote(zout.at[j], zin.at[j], qs.at[j], qr.at[j], zy(d, 0))
 
     for j, d in enumerate((1, 1, 2, 4)):
-        zout[j, 0:4] = acc
-        zout[j, 4] = dec
+        if j == 3:
+            far_out[...] = acc.astype(BF16)
+        else:
+            zout[j, 0:4] = acc
+            zout[j, 4] = dec
         z_round(j, d).start()
         kv_step(5 + j)
         for dz in ((), (2,), (3, 4), (5, 6))[j]:
@@ -263,6 +278,9 @@
             attend_plane(7)
         z_round(j, d).wait_recv()
         here = (z >= d).astype(F32)
+        if j == 3:
+            acc = acc + jnp.exp2(rate * dec[None]) * (far_in[...].astype(F32) * here)
+            continue
         got = zin[j, 0:4] * here
         got_dec = zin[j, 4] * here
         if j == 0:
@@ -346,13 +364,13 @@
             pltpu.VMEM((32, TOK), F32),
             pltpu.SMEM((32, TOK), F32),
             pltpu.VMEM((16, 16, 128), F32),
-            pltpu.VMEM((GROUP, 16, 128), F32),
+            pltpu.VMEM((TOK, 16, 128), F32),
             pltpu.VMEM((TOK, 16, 128), F32),
             pltpu.VMEM((TOK, 16, 16, 128), F32),
             pltpu.VMEM((YN, 5, 16, 128), F32),
             pltpu.VMEM((YN, 5, 16, 128), F32),
-            pltpu.VMEM((4, 5, 16, 128), F32),
-            pltpu.VMEM((4, 5, 16, 128), F32),
+            pltpu.VMEM((3, 5, 16, 128), F32),
+            pltpu.VMEM((3, 5, 16, 128), F32),
             pltpu.VMEM((YN, 4, 16, 128), F32),
             pltpu.VMEM((YN, 4, 16, 128), F32),
             pltpu.VMEM((GROUP, 16, 128), F32),
@@ -362,6 +380,8 @@
             pltpu.VMEM((128, 1024), F32),
             pltpu.VMEM((128, 1024), BF16),
             pltpu.VMEM((128, PLANE), BF16),
+            pltpu.VMEM((4, 16, 128), BF16),
+            pltpu.VMEM((4, 16, 128), BF16),
             dma((2,)),
             dma(()),
         ]

time: 65.9 us -> 64.9 us (0.985)
  the two profiles are of different devices: /device:TPU:4 before, /device:TPU:8 now
where the time goes in v5:
time: 64.9 us; the launch traced here: 64.7 us
  Pallas kernels  64.1 us (99%)
    pallas_call x1, Pallas kernels, main_pass(): pl.pallas_call(main_kernel, out_shape=(jax.ShapeDtypeStruct((1024, 128),...  61.9 us
    pallas_call x1, Pallas kernels, finish(): pl.pallas_call(finish_kernel, out_shape=tuple((jax.ShapeDtypeStruct(v.sha...  2.22 us

profile of v5, /device:TPU:8, one launch (start us, length us, event | category | flops | bytes accessed | tf_op | source)
XLA Modules:
  0.0 64.7 jit_solution(652565263933025488)
XLA Ops:
  0.6 61.9 %layer.1 = (bf16[1024,128]{1,0:T(8,128)(2,1)}, bf16[128,2048]{1,0:T(8,128)(2,1)}) custom-call(s32[4]{0:T(128)} %len_ref.3, bf16[128,128]{1,0:T(8,128)(2,1)} %bitcast.7, bf16[128,128]{1,0:T(8,128)(2,1)} %bitcast.8, bf16[128,2048]{1,0:T(8,128)(2,1)} %x_ref.1, bf16[32,2048]{1,0:T(8,128)(2,1)} %w_ref.1, bf16[128,2048]{1,0:T(8,128)(2,1)} %dt_ref.1, ...), custom_call_target="tpu_custom_call" | custom-call | tf_op jit(solution)/shard_map/layer/pallas_call | solution.py:353
  62.5 2.2 %steer_finish.1 = (bf16[1024,128]{1,0:T(8,128)(2,1)}, bf16[128,2048]{1,0:T(8,128)(2,1)}, bf16[128,1024]{1,0:T(8,128)(2,1)}) custom-call(s32[4]{0:T(128)} %len_ref.3, s32[4]{0:T(128)} %idx_ref.1, s32[4]{0:T(128)} %num_ref.1, bf16[1024,128]{1,0:T(8,128)(2,1)} %get-tuple-element.8.ctx_ref, bf16[128,2048]{1,0:T(8,128)(2,1)} %get-tuple-element.9.mix_ref, ...), custom_call_target="tpu_custom_call" | custom-call | tf_op jit(solution)/shard_map/steer_finish/pallas_call | solution.py:416
